TPU v7x, 256 devices: a whole 4x4x8 slice. The times are simulated.
256 devices in a mesh: gx: 16 (over y, z_hi), gy: 16 (over x, z_lo, core).
Axes of the slice: x: 4, y: 4, z: 8 (z_hi: 4, z_lo: 2; z = z_hi * 2 + z_lo), core: 2. Of those that a mesh axis runs over, the one named last changes fastest.
Arguments:
- signal: bfloat16 [131072, 384], P(('gx', 'gy')), may hold values from -6 to 6
- w_up: bfloat16 [768, 1536], replicated, may hold values from -0.21875 to 0.21875
- w_down: bfloat16 [768, 1536], replicated, may hold values from -0.15625 to 0.15625
- cotangent: bfloat16 [131072, 384], P(('gx', 'gy')), may hold values from -0.016479492 to 0.016479492
Outputs:
- mixed_out: bfloat16 [131072, 384], P(('gx', 'gy'))
- grad_up: float32 [768, 1536], P('gx', 'gy')
- grad_down: float32 [768, 1536], P('gx', 'gy')
All inputs are finite; a program needn't handle non-finite values.
Results may differ from a plain program's by a relative error of at most 0.023.
Values may be sent and summed in bfloat16 or wider, within the bound.
A program may use at most 128 MiB of HBM per device.

v0:
```python
import math

import jax
import jax.numpy as jnp
from jax import lax
from jax.sharding import PartitionSpec as P


def swapped(value, axis, distance):
    mask = 2**distance
    pairs = [(source, source ^ mask) for source in range(lax.axis_size(axis))]
    return lax.ppermute(value, axis, pairs)


def normalize(pair):
    values = pair.astype(jnp.float32)
    centre = jnp.mean(values, axis=-1, keepdims=True)
    shifted = values - centre
    spread = jnp.mean(shifted * shifted, axis=-1, keepdims=True)
    factor = lax.rsqrt(spread + 1e-05)
    return (shifted * factor, factor)


def gelu_value(pre):
    return 0.5 * pre * (1.0 + lax.erf(pre * (1.0 / math.sqrt(2.0))))


def gelu_slope(pre):
    return 0.5 * (1.0 + lax.erf(pre * (1.0 / math.sqrt(2.0)))) + pre * jnp.exp(-0.5 * pre * pre) * (
        1.0 / math.sqrt(2.0 * math.pi)
    )


def contract_last(left, right):
    return lax.dot_general(
        left, right, (((1,), (1,)), ((), ())), preferred_element_type=jnp.float32
    )


def contract_first(left, right):
    return lax.dot_general(
        left, right, (((0,), (0,)), ((), ())), preferred_element_type=jnp.float32
    )


def switch_forward(pair, w_up, w_down):
    normed, factor = normalize(pair)
    normed_bf = normed.astype(jnp.bfloat16)
    pre = jnp.dot(normed_bf, w_up, preferred_element_type=jnp.float32)
    hidden = gelu_value(pre).astype(jnp.bfloat16)
    mixed = pair.astype(jnp.float32) + contract_last(hidden, w_down)
    return (mixed.astype(jnp.bfloat16), pre)


def switch_backward(pair, pre, pair_grad, w_up, w_down, need_input):
    normed, factor = normalize(pair)
    normed_bf = normed.astype(jnp.bfloat16)
    hidden = gelu_value(pre).astype(jnp.bfloat16)
    d_hidden = jnp.dot(pair_grad, w_down, preferred_element_type=jnp.float32)
    grad_down = contract_first(pair_grad, hidden)
    d_pre = (d_hidden * gelu_slope(pre)).astype(jnp.bfloat16)
    grad_up = contract_first(normed_bf, d_pre)
    d_input = None
    if need_input:
        d_norm = contract_last(d_pre, w_up)
        d_pair = factor * (
            d_norm
            - jnp.mean(d_norm, axis=-1, keepdims=True)
            - normed * jnp.mean(d_norm * normed, axis=-1, keepdims=True)
        )
        d_input = (pair_grad.astype(jnp.float32) + d_pair).astype(jnp.bfloat16)
    return (grad_up, grad_down, d_input)


def there_gx(block, bit):
    return swapped(block, "gx", bit)


def back_gx(block, bit):
    return swapped(block, "gx", bit)


def there_gy(block, bit):
    return swapped(block, "gy", bit)


def back_gy(block, bit):
    return swapped(block, "gy", bit)


def join_pair(lower, mine, theirs):
    return jnp.where(lower, jnp.concatenate([mine, theirs], 1), jnp.concatenate([theirs, mine], 1))


def split_halves(lower, block):
    half = block.shape[0] // 2
    first, second = (block[:half], block[half:])
    return (jnp.where(lower, first, second), jnp.where(lower, second, first))


def return_halves(lower, bit, pairs, bring):
    width = pairs.shape[1] // 2
    low_part, high_part = (pairs[:, :width], pairs[:, width:])
    returned = bring(jnp.where(lower, high_part, low_part), bit)
    mine = jnp.where(lower, low_part, high_part)
    return jnp.where(
        lower, jnp.concatenate([mine, returned], 0), jnp.concatenate([returned, mine], 0)
    )


def halves_forward(state, lower, bit, send, bring, w_up, w_down):
    keep, give = split_halves(lower, state)
    pair = join_pair(lower, keep, send(give, bit))
    mixed, pre = switch_forward(pair, w_up, w_down)
    return (return_halves(lower, bit, mixed, bring), (pair, pre))


def halves_backward(grad, lower, bit, send, bring, saved, need_input, w_up, w_down):
    keep, give = split_halves(lower, grad)
    pair_grad = join_pair(lower, keep, send(give, bit))
    part_up, part_down, d_input = switch_backward(
        saved[0], saved[1], pair_grad, w_up, w_down, need_input
    )
    new_grad = None
    if need_input:
        new_grad = return_halves(lower, bit, d_input, bring)
    return (new_grad, part_up, part_down)


def local(signal, w_up, w_down, cotangent):
    span_x = lax.axis_size("gx")
    span_y = lax.axis_size("gy")
    bits_x = [span_x.bit_length() - 2, 0]
    bits_y = [span_y.bit_length() - 2, 0]
    total_up = jnp.zeros(w_up.shape, jnp.float32)
    total_down = jnp.zeros(w_down.shape, jnp.float32)
    index_x = lax.axis_index("gx")
    index_y = lax.axis_index("gy")
    plan = []
    for bit in bits_x:
        plan.append((index_x // (1 << bit) % 2 == 0, bit, there_gx, back_gx))
    for bit in bits_y:
        plan.append((index_y // (1 << bit) % 2 == 0, bit, there_gy, back_gy))
    state = signal
    saved = []
    for lower, bit, send, bring in plan:
        state, kept = halves_forward(state, lower, bit, send, bring, w_up, w_down)
        saved.append(kept)
    grad = cotangent
    for section in [3, 2, 1, 0]:
        lower, bit, send, bring = plan[section]
        grad, part_up, part_down = halves_backward(
            grad, lower, bit, send, bring, saved[section], section > 0, w_up, w_down
        )
        total_up = total_up + part_up
        total_down = total_down + part_down
    partial_up, partial_down = (
        lax.psum_scatter(
            total_up.astype(jnp.bfloat16), "gx", scatter_dimension=0, tiled=True
        ).astype(jnp.float32),
        lax.psum_scatter(
            total_down.astype(jnp.bfloat16), "gx", scatter_dimension=0, tiled=True
        ).astype(jnp.float32),
    )
    grad_up, grad_down = (
        lax.psum_scatter(
            partial_up.astype(jnp.bfloat16), "gy", scatter_dimension=1, tiled=True
        ).astype(jnp.float32),
        lax.psum_scatter(
            partial_down.astype(jnp.bfloat16), "gy", scatter_dimension=1, tiled=True
        ).astype(jnp.float32),
    )
    return (state, grad_up, grad_down)


def solution(mesh):
    return jax.shard_map(
        local,
        mesh=mesh,
        in_specs=(P(("gx", "gy"), None), P(), P(), P(("gx", "gy"), None)),
        out_specs=(P(("gx", "gy"), None), P("gx", "gy"), P("gx", "gy")),
        check_vma=False,
    )
```

profile of v0, /device:TPU:1, one launch (start us, length us, event | category | flops | bytes accessed | tf_op | source)
XLA Modules:
  0.0 463.2 jit_solution(6215154174066619682)
XLA Ops:
  8.5 3.8 collective-permute-start
  12.3 3.6 collective-permute-done
  20.1 3.8 collective-permute-start.1
  23.9 3.1 collective-permute-done.1
  27.1 3.5 collective-permute-start.2
  30.6 8.2 %collective-permute-done.2 = bf16[256,384]{1,0:T(8,128)(2,1)S(1)} collective-permute-done((bf16[256,384]{1,0:T(8,128)(2,1)S(1)}, bf16[256,384]{1,0:T(8,128)(2,1)S(1)}, u32[]{:S(2)}, u32[]{:S(2)}) %collective-permute-start.2) | collective-permute-done | bytes 196640 | tf_op jit(solution)/shard_map/ppermute | solution.py:12
  39.4 2.1 multiply_convert_fusion.2
  43.1 10.6 %collective-permute-done.3 = bf16[256,384]{1,0:T(8,128)(2,1)S(1)} collective-permute-done((bf16[256,384]{1,0:T(8,128)(2,1)}, bf16[256,384]{1,0:T(8,128)(2,1)S(1)}, u32[]{:S(2)}, u32[]{:S(2)}) %collective-permute-start.3) | collective-permute-done | bytes 196640 | tf_op jit(solution)/shard_map/ppermute | solution.py:12
  55.6 2.8 collective-permute-start.4
  58.4 3.3 collective-permute-done.4
  62.2 2.1 multiply_convert_fusion.1
  65.2 2.8 collective-permute-start.5
  68.0 3.4 collective-permute-done.5
  72.6 4.4 collective-permute-start.6
  84.4 2.8 collective-permute-start.10
  87.2 4.8 %collective-permute-done.10 = bf16[256,384]{1,0:T(8,128)(2,1)S(1)} collective-permute-done((bf16[256,384]{1,0:T(8,128)(2,1)S(1)}, bf16[256,384]{1,0:T(8,128)(2,1)S(1)}, u32[]{:S(2)}, u32[]{:S(2)}) %collective-permute-start.10) | collective-permute-done | bytes 196640 | tf_op jit(solution)/shard_map/ppermute | solution.py:12
  94.5 2.8 collective-permute-start.11
  97.3 4.0 collective-permute-done.11
  101.6 3.1 fusion.71
  104.7 8.1 %collective-permute-done.12 = bf16[256,384]{1,0:T(8,128)(2,1)S(1)} collective-permute-done((bf16[256,384]{1,0:T(8,128)(2,1)S(1)}, bf16[256,384]{1,0:T(8,128)(2,1)S(1)}, u32[]{:S(2)}, u32[]{:S(2)}) %collective-permute-start.12) | collective-permute-done | bytes 196640 | tf_op jit(solution)/shard_map/ppermute | solution.py:12
  115.2 3.2 fusion.75
  118.4 8.0 %collective-permute-done.13 = bf16[256,384]{1,0:T(8,128)(2,1)S(1)} collective-permute-done((bf16[256,384]{1,0:T(8,128)(2,1)S(1)}, bf16[256,384]{1,0:T(8,128)(2,1)S(1)}, u32[]{:S(2)}, u32[]{:S(2)}) %collective-permute-start.13) | collective-permute-done | bytes 196640 | tf_op jit(solution)/shard_map/ppermute | solution.py:12
  126.6 3.2 collective-permute-start.14
  129.8 3.1 fusion.79
  134.4 9.1 %add_convert_fusion.1 = bf16[768,1536]{1,0:T(8,128)(2,1)} fusion(f32[768,1536]{1,0:T(8,128)} %fusion.79, f32[768,1536]{1,0:T(8,128)} %fusion.71, f32[768,1536]{1,0:T(8,128)} %fusion.75, bf16[768,1536]{1,0:T(8,128)(2,1)} %param.6, f32[256,1536]{1,0:T(8,128)S(1)} %copy-done.3, bf16[256,384]{1,0:T(8,128)(2,1)S(1)} %collective-permute-done.14, ...), kind=kOutput, calls=%fused_computation.1 | convolution fusion | flops 1220935680 | bytes 21235712 | tf_op jit(solution)/shard_map/dot_general | solution.py:41
  148.7 2.4 add_convert_fusion
  151.1 85.9 %reduce-scatter.9.cloned.1.call-done = bf16[48,1536]{1,0:T(8,128)(2,1)} async-done(((bf16[768,1536]{1,0:T(8,128)(2,1)}), bf16[48,1536]{1,0:T(8,128)(2,1)}) %reduce-scatter.9.cloned.1.call-update) | async-done | bytes 147472 | tf_op jit(solution)/shard_map/reduce_scatter | solution.py:158
  238.9 2.9 fusion.23
  241.8 2.4 collective-permute-start.7
  244.3 84.3 %reduce-scatter.11.cloned.1.call-done = bf16[48,1536]{1,0:T(8,128)(2,1)} async-done(((bf16[768,1536]{1,0:T(8,128)(2,1)}), bf16[48,1536]{1,0:T(8,128)(2,1)}) %reduce-scatter.11.cloned.1.call-update) | async-done | bytes 147472 | tf_op jit(solution)/shard_map/reduce_scatter | solution.py:161
  331.3 59.8 %reduce-scatter.13.cloned.1.call-done = bf16[96,48]{1,0:T(8,128)(2,1)} async-done(((bf16[1536,48]{1,0:T(8,128)(2,1)}), bf16[96,48]{1,0:T(8,128)(2,1)}) %reduce-scatter.13.cloned.1.call-update) | async-done | bytes 9232
  392.6 62.7 %reduce-scatter.15.cloned.1.call-done = bf16[96,48]{1,0:T(8,128)(2,1)} async-done(((bf16[1536,48]{1,0:T(8,128)(2,1)}), bf16[96,48]{1,0:T(8,128)(2,1)}) %reduce-scatter.15.cloned.1.call-update) | async-done | bytes 9232
  (156 shorter events, 38.9 us)
Async XLA Ops:
  7.2 10.0 %copy-start = (bf16[768,1536]{1,0:T(8,128)(2,1)S(1)}, bf16[768,1536]{1,0:T(8,128)(2,1)}, u32[]{:S(2)}) copy-start(bf16[768,1536]{1,0:T(8,128)(2,1)} %param.5) | copy-start | bytes 7077892
  7.2 229.8 %reduce-scatter.9.cloned.1.call-start = ((), (), s32[]{:S(2)}) async-start(), calls=%async_computation.4 | async-start | bytes 2506752 | tf_op jit(solution)/shard_map/reduce_scatter | solution.py:158
  8.5 7.4 %collective-permute-start = (bf16[256,384]{1,0:T(8,128)(2,1)S(1)}, bf16[256,384]{1,0:T(8,128)(2,1)S(1)}, u32[]{:S(2)}, u32[]{:S(2)}) collective-permute-start(bf16[256,384]{1,0:T(8,128)(2,1)S(1)} %get-tuple-element.37), channel_id=1, source_target_pairs={{0,128},{16,144},{32,160},{48,176},{64,192},{80,208},{96,224},{112... | collective-permute-start | bytes 589832 | tf_op jit(solution)/shard_map/ppermute | solution.py:12
  20.1 6.9 %collective-permute-start.1 = (bf16[256,384]{1,0:T(8,128)(2,1)S(1)}, bf16[256,384]{1,0:T(8,128)(2,1)S(1)}, u32[]{:S(2)}, u32[]{:S(2)}) collective-permute-start(bf16[256,384]{1,0:T(8,128)(2,1)S(1)} %get-tuple-element.36), channel_id=1, source_target_pairs={{0,128},{16,144},{32,160},{48,176},{64,192},{80,208},{96,224},{112... | collective-permute-start | bytes 589832 | tf_op jit(solution)/shard_map/ppermute | solution.py:12
  27.1 11.8 %collective-permute-start.2 = (bf16[256,384]{1,0:T(8,128)(2,1)S(1)}, bf16[256,384]{1,0:T(8,128)(2,1)S(1)}, u32[]{:S(2)}, u32[]{:S(2)}) collective-permute-start(bf16[256,384]{1,0:T(8,128)(2,1)S(1)} %get-tuple-element.33), channel_id=1, source_target_pairs={{0,16},{16,0},{32,48},{48,32},{64,80},{80,64},{96,112},{112,96},{1... | collective-permute-start | bytes 589832 | tf_op jit(solution)/shard_map/ppermute | solution.py:12
  43.1 10.6 %collective-permute-start.3 = (bf16[256,384]{1,0:T(8,128)(2,1)}, bf16[256,384]{1,0:T(8,128)(2,1)S(1)}, u32[]{:S(2)}, u32[]{:S(2)}) collective-permute-start(bf16[256,384]{1,0:T(8,128)(2,1)} %get-tuple-element.32), channel_id=1, source_target_pairs={{0,16},{16,0},{32,48},{48,32},{64,80},{80,64},{96,112},{112,96},{1... | collective-permute-start | bytes 589832 | tf_op jit(solution)/shard_map/ppermute | solution.py:12
  55.6 6.1 %collective-permute-start.4 = (bf16[256,384]{1,0:T(8,128)(2,1)S(1)}, bf16[256,384]{1,0:T(8,128)(2,1)S(1)}, u32[]{:S(2)}, u32[]{:S(2)}) collective-permute-start(bf16[256,384]{1,0:T(8,128)(2,1)S(1)} %get-tuple-element.29), channel_id=1, source_target_pairs={{0,8},{1,9},{2,10},{3,11},{4,12},{5,13},{6,14},{7,15},{8,0},{9,1},... | collective-permute-start | bytes 589832 | tf_op jit(solution)/shard_map/ppermute | solution.py:12
  61.7 2.6 copy-start.4
  65.2 6.2 %collective-permute-start.5 = (bf16[256,384]{1,0:T(8,128)(2,1)S(1)}, bf16[256,384]{1,0:T(8,128)(2,1)}, u32[]{:S(2)}, u32[]{:S(2)}) collective-permute-start(bf16[256,384]{1,0:T(8,128)(2,1)S(1)} %get-tuple-element.28), channel_id=1, source_target_pairs={{0,8},{1,9},{2,10},{3,11},{4,12},{5,13},{6,14},{7,15},{8,0},{9,1},... | collective-permute-start | bytes 589832 | tf_op jit(solution)/shard_map/ppermute | solution.py:12
  68.0 9.0 %copy-start.28 = (bf16[512,384]{1,0:T(8,128)(2,1)S(1)}, bf16[512,384]{1,0:T(8,128)(2,1)}, u32[]{:S(2)}) copy-start(bf16[512,384]{1,0:T(8,128)(2,1)} %param.7) | copy-start | bytes 1179652
  72.6 5.5 %collective-permute-start.6 = (bf16[256,384]{1,0:T(8,128)(2,1)S(1)}, bf16[256,384]{1,0:T(8,128)(2,1)S(1)}, u32[]{:S(2)}, u32[]{:S(2)}) collective-permute-start(bf16[256,384]{1,0:T(8,128)(2,1)S(1)} %get-tuple-element.25), channel_id=1, source_target_pairs={{0,1},{1,0},{2,3},{3,2},{4,5},{5,4},{6,7},{7,6},{8,9},{9,8},{10,11... | collective-permute-start | bytes 589832 | tf_op jit(solution)/shard_map/ppermute | solution.py:12
  77.0 5.2 %copy-start.12 = (bf16[256,384]{1,0:T(8,128)(2,1)}, bf16[256,384]{1,0:T(8,128)(2,1)S(1)}, u32[]{:S(2)}) copy-start(bf16[256,384]{1,0:T(8,128)(2,1)S(1)} %get-tuple-element.21) | copy-start | bytes 589828
  77.0 3.3 collective-permute-start.8
  82.6 9.5 %copy-start.35 = (f32[256,1536]{1,0:T(8,128)S(1)}, f32[256,1536]{1,0:T(8,128)}, u32[]{:S(2)}) copy-start(f32[256,1536]{1,0:T(8,128)} %get-tuple-element.42) | copy-start | bytes 4718596
  82.7 1.5 collective-permute-start.9
  84.4 9.7 %copy-start.14 = (bf16[256,384]{1,0:T(8,128)(2,1)}, bf16[256,384]{1,0:T(8,128)(2,1)S(1)}, u32[]{:S(2)}) copy-start(bf16[256,384]{1,0:T(8,128)(2,1)S(1)} %get-tuple-element.17) | copy-start | bytes 589828
  84.4 7.7 %collective-permute-start.10 = (bf16[256,384]{1,0:T(8,128)(2,1)S(1)}, bf16[256,384]{1,0:T(8,128)(2,1)S(1)}, u32[]{:S(2)}, u32[]{:S(2)}) collective-permute-start(bf16[256,384]{1,0:T(8,128)(2,1)S(1)} %get-tuple-element.18), channel_id=1, source_target_pairs={{0,8},{1,9},{2,10},{3,11},{4,12},{5,13},{6,14},{7,15},{8,0},{9,1},... | collective-permute-start | bytes 589832 | tf_op jit(solution)/shard_map/ppermute | solution.py:12
  94.5 6.8 %collective-permute-start.11 = (bf16[256,384]{1,0:T(8,128)(2,1)S(1)}, bf16[256,384]{1,0:T(8,128)(2,1)S(1)}, u32[]{:S(2)}, u32[]{:S(2)}) collective-permute-start(bf16[256,384]{1,0:T(8,128)(2,1)S(1)} %get-tuple-element.16), channel_id=1, source_target_pairs={{0,8},{1,9},{2,10},{3,11},{4,12},{5,13},{6,14},{7,15},{8,0},{9,1},... | collective-permute-start | bytes 589832 | tf_op jit(solution)/shard_map/ppermute | solution.py:12
  101.5 13.2 %copy-start.16 = (bf16[256,384]{1,0:T(8,128)(2,1)}, bf16[256,384]{1,0:T(8,128)(2,1)S(1)}, u32[]{:S(2)}) copy-start(bf16[256,384]{1,0:T(8,128)(2,1)S(1)} %get-tuple-element.13) | copy-start | bytes 589828
  101.5 11.3 %copy-start.34 = (f32[256,1536]{1,0:T(8,128)S(1)}, f32[256,1536]{1,0:T(8,128)}, u32[]{:S(2)}) copy-start(f32[256,1536]{1,0:T(8,128)} %get-tuple-element.40) | copy-start | bytes 4718596
  101.5 11.3 %collective-permute-start.12 = (bf16[256,384]{1,0:T(8,128)(2,1)S(1)}, bf16[256,384]{1,0:T(8,128)(2,1)S(1)}, u32[]{:S(2)}, u32[]{:S(2)}) collective-permute-start(bf16[256,384]{1,0:T(8,128)(2,1)S(1)} %get-tuple-element.14), channel_id=1, source_target_pairs={{0,16},{16,0},{32,48},{48,32},{64,80},{80,64},{96,112},{112,96},{1... | collective-permute-start | bytes 589832 | tf_op jit(solution)/shard_map/ppermute | solution.py:12
  115.1 11.2 %collective-permute-start.13 = (bf16[256,384]{1,0:T(8,128)(2,1)S(1)}, bf16[256,384]{1,0:T(8,128)(2,1)S(1)}, u32[]{:S(2)}, u32[]{:S(2)}) collective-permute-start(bf16[256,384]{1,0:T(8,128)(2,1)S(1)} %get-tuple-element.12), channel_id=1, source_target_pairs={{0,16},{16,0},{32,48},{48,32},{64,80},{80,64},{96,112},{112,96},{1... | collective-permute-start | bytes 589832 | tf_op jit(solution)/shard_map/ppermute | solution.py:12
  126.6 7.8 %copy-start.3 = (f32[256,1536]{1,0:T(8,128)S(1)}, f32[256,1536]{1,0:T(8,128)}, u32[]{:S(2)}) copy-start(f32[256,1536]{1,0:T(8,128)} %copy-done.2) | copy-start | bytes 4718596
  126.6 7.8 %copy-start.11 = (bf16[256,384]{1,0:T(8,128)(2,1)S(1)}, bf16[256,384]{1,0:T(8,128)(2,1)}, u32[]{:S(2)}) copy-start(bf16[256,384]{1,0:T(8,128)(2,1)} %copy-done.10) | copy-start | bytes 589828
  126.6 7.8 %copy-start.31 = (f32[256]{0:T(256)S(1)}, f32[256]{0:T(256)}, u32[]{:S(2)}) copy-start(f32[256]{0:T(256)} %copy-done.30) | copy-start | bytes 3076
  126.6 7.8 %copy-start.33 = (f32[256]{0:T(256)S(1)}, f32[256]{0:T(256)}, u32[]{:S(2)}) copy-start(f32[256]{0:T(256)} %copy-done.32) | copy-start | bytes 3076
  126.6 7.8 %collective-permute-start.14 = (bf16[256,384]{1,0:T(8,128)(2,1)S(1)}, bf16[256,384]{1,0:T(8,128)(2,1)S(1)}, u32[]{:S(2)}, u32[]{:S(2)}) collective-permute-start(bf16[256,384]{1,0:T(8,128)(2,1)S(1)} %get-tuple-element.10), channel_id=1, source_target_pairs={{0,128},{16,144},{32,160},{48,176},{64,192},{80,208},{96,224},{112... | collective-permute-start | bytes 589832 | tf_op jit(solution)/shard_map/ppermute | solution.py:12
  143.5 185.0 %reduce-scatter.11.cloned.1.call-start = ((), (), s32[]{:S(2)}) async-start(), calls=%async_computation.5 | async-start | bytes 2506752 | tf_op jit(solution)/shard_map/reduce_scatter | solution.py:161
  151.1 240.1 %reduce-scatter.13.cloned.1.call-start = ((), (), s32[]{:S(2)}) async-start(), calls=%async_computation.6 | async-start | bytes 417792
  238.9 216.4 %reduce-scatter.15.cloned.1.call-start = ((), (), s32[]{:S(2)}) async-start(), calls=%async_computation.7 | async-start | bytes 417792
  238.9 217.8 %copy-start.1 = (bf16[768,1536]{1,0:T(8,128)(2,1)S(1)}, bf16[768,1536]{1,0:T(8,128)(2,1)}, u32[]{:S(2)}) copy-start(bf16[768,1536]{1,0:T(8,128)(2,1)} %param.5) | copy-start | bytes 7077892
  241.8 88.6 %collective-permute-start.7 = (bf16[256,384]{1,0:T(8,128)(2,1)S(1)}, bf16[256,384]{1,0:T(8,128)(2,1)S(1)}, u32[]{:S(2)}, u32[]{:S(2)}) collective-permute-start(bf16[256,384]{1,0:T(8,128)(2,1)S(1)} %get-tuple-element.24), channel_id=1, source_target_pairs={{0,1},{1,0},{2,3},{3,2},{4,5},{5,4},{6,7},{7,6},{8,9},{9,8},{10,11... | collective-permute-start | bytes 589832 | tf_op jit(solution)/shard_map/ppermute | solution.py:12
  (23 other events, 32.9 us)
Sparse Core Ops, SparseCore 0:
  143.6 93.3 reduce-scatter.8
  240.6 87.9 reduce-scatter.10
  331.0 60.0 reduce-scatter.12
  393.5 61.7 reduce-scatter.14
where the time goes:
time: 466 us; the launch traced here: 463 us
  waiting for transfers between devices  353 us (76%)
  matrix products  42.2 us (9%)
  starting transfers between devices  33.6 us (7%)
  between operations  14.4 us (3%)
  other arithmetic  10.5 us (2%)
  local copies, waits for them, and re-layouts  9.61 us (2%)
    unnamed x6, waiting for transfers between devices  123 us
    reduce_scatter x1, waiting for transfers between devices, local(): lax.psum_scatter(total_up.astype(jnp.bfloat16), 'gx', scatter_dimension=0...  85.9 us
    reduce_scatter x1, waiting for transfers between devices, local(): lax.psum_scatter(total_down.astype(jnp.bfloat16), 'gx', scatter_dimension...  84.3 us
    ppermute x15, waiting for transfers between devices, swapped(): return lax.ppermute(value, axis, pairs)  60.3 us
    ppermute x15, starting transfers between devices, swapped(): return lax.ppermute(value, axis, pairs)  33.5 us
    dot_general x8, matrix products, contract_first(): lax.dot_general(left, right, (((0,), (0,)), ((), ())), preferred_element_...  24.5 us
    unnamed x76, local copies, waits for them, and re-layouts  9.61 us
  transfers between devices with their start and end apart: 19, of which 17 were waited for; matrix products, arithmetic and copies ran while one was open for 6% of the time, Pallas kernels for 0%

commit v1 on v0

v1 whole, which is shorter than its diff:
```python
import math

import jax
import jax.numpy as jnp
from jax import lax
from jax.experimental import pallas as pl
from jax.experimental.pallas import tpu as pltpu
from jax.sharding import PartitionSpec as P

MESH = pl.DeviceIdType.MESH
BF = jnp.bfloat16
F32 = jnp.float32
D = 384
D2 = 768
FF = 1536
CH = 32
ROWS = 256
TILE = 256


def dot_nn(left, right):
    return lax.dot_general(left, right, (((1,), (0,)), ((), ())), preferred_element_type=F32)


def dot_nt(left, right):
    return lax.dot_general(left, right, (((1,), (1,)), ((), ())), preferred_element_type=F32)


def kernel(
    sig, cot, wu_hbm, wd_hbm, mixed, gout,
    xs, gs, nbv, gpv, nf, rs, slope, wu, wd, acc, lk, rk, m4, ay, bx, fz, ft,
    sa1, ra1, sa2, ra2, sx1, rx1, sx2, rx2, sb1, rb1, sb2, rb2, sy1, ry1, sy2, ry2, zr, pt, tt,
    sig_s, sig_r, cot_s, cot_r, mix_s, mix_r, loc, lk_s, lk_r, rk_s, rk_r, red_s, red_r,
):
    gx = lax.axis_index("gx")
    gy = lax.axis_index("gy")
    y, zh = gx // 4, gx % 4
    x, zl, c = gy // 4, (gy // 2) % 2, gy % 2
    z = zh * 2 + zl
    ba, bb, bc = y // 2, zh % 2, x // 2
    me = ba * 8 + bb * 4 + bc * 2 + c

    def at(xx, yy, zz, cc):
        return {"gx": yy * 4 + zz // 2, "gy": xx * 4 + (zz % 2) * 2 + cc}

    yp, ym, y2 = (y + 1) % 4, (y + 3) % 4, (y + 2) % 4
    xp, xm = (x + 1) % 4, (x + 3) % 4
    ydev = (at(x, yp, z, c), at(x, ym, z, c))
    xdev = (at(xp, y, z, c), at(xm, y, z, c))
    zdev = [at(x, y, (z + d) % 8, c) for d in range(1, 8)]
    other = at(x, y, z, 1 - c)
    group = []
    for r in range(1, 16):
        ra, rb, rc, rd = r // 8, (r // 4) % 2, (r // 2) % 2, r % 2
        yy = y + ra * (2 - 4 * ba)
        zz = z + rb * (2 - 4 * bb)
        xx = x + rc * (2 - 4 * bc)
        cc = c + rd * (1 - 2 * c)
        target = (yy // 2) * 8 + ((zz // 2) % 2) * 4 + (xx // 2) * 2 + cc
        group.append((r, at(xx, yy, zz, cc), target))

    load_wu = pltpu.make_async_copy(wu_hbm, wu, loc.at[0])
    load_wd = pltpu.make_async_copy(wd_hbm, wd, loc.at[1])
    load_wu.start()
    load_wd.start()
    own_rows = pl.ds(pl.multiple_of(me * CH, CH), CH)
    own_sig = pltpu.make_async_copy(sig.at[own_rows], xs.at[me], loc.at[2])
    own_cot = pltpu.make_async_copy(cot.at[own_rows], gs.at[me], loc.at[3])
    own_sig.start()
    own_cot.start()

    barrier = pltpu.get_barrier_semaphore()
    peers = [dev for _, dev, _ in group] + zdev + list(ydev) + list(xdev)
    for dev in peers:
        pl.semaphore_signal(barrier, inc=1, device_id=dev, device_id_type=MESH)
    pl.semaphore_wait(barrier, len(peers))

    def remote(src, dst, send, recv, dev):
        return pltpu.make_async_remote_copy(
            src_ref=src, dst_ref=dst, send_sem=send, recv_sem=recv, device_id=dev, device_id_type=MESH
        )

    sig_copies, cot_copies = [], []
    for r, dev, target in reversed(group):
        rows = pl.ds(pl.multiple_of(target * CH, CH), CH)
        sig_copies.append(remote(sig.at[rows], xs.at[me], sig_s.at[r], sig_r.at[r], dev))
        cot_copies.append(remote(cot.at[rows], gs.at[me], cot_s.at[r], cot_r.at[r], dev))
    for copy in sig_copies:
        copy.start()
    for copy in cot_copies:
        copy.start()
    load_wu.wait()
    load_wd.wait()
    own_sig.wait()
    for copy in sig_copies:
        copy.wait()

    def low_high(k, i):
        stride = 8 >> k
        low = (i // stride) * 2 * stride + i % stride
        return low, low + stride

    def send_left(k):
        cols = pl.ds(k * ROWS, ROWS)
        into = pl.ds(4 * ROWS + k * ROWS, ROWS)
        return remote(lk.at[1 - c, :, cols], lk.at[1 - c, :, into], lk_s.at[k], lk_r.at[k], other)

    def send_right(k):
        cols = pl.ds(k * ROWS, ROWS)
        into = pl.ds(4 * ROWS + k * ROWS, ROWS)
        return remote(rk.at[1 - c, cols], rk.at[1 - c, into], rk_s.at[k], rk_r.at[k], other)

    for k in range(4):
        for i in range(8):
            low, high = low_high(k, i)
            rows = pl.ds(i * CH, CH)
            pair = jnp.concatenate([xs[low], xs[high]], axis=1).astype(F32)
            centre = jnp.mean(pair, axis=-1, keepdims=True)
            shifted = pair - centre
            spread = jnp.mean(shifted * shifted, axis=-1, keepdims=True)
            factor = lax.rsqrt(spread + 1e-05)
            normed = shifted * factor
            nf[k, rows] = normed
            rs[k, rows] = factor
            nbv[rows] = normed.astype(BF)
        lk[0, :, k * ROWS : (k + 1) * ROWS] = nbv[...].T

        @pl.when(c == 1)
        def _():
            send_left(k).start()

        for j in range(FF // TILE):
            cols = slice(j * TILE, (j + 1) * TILE)
            pre = dot_nn(nbv[...], wu[:, cols])
            half = 0.5 * (1.0 + lax.erf(pre * (1.0 / math.sqrt(2.0))))
            rk[1, k * ROWS : (k + 1) * ROWS, cols] = (pre * half).astype(BF)
            slope[k, :, cols] = half + pre * jnp.exp(-0.5 * pre * pre) * (1.0 / math.sqrt(2.0 * math.pi))

        @pl.when(c == 0)
        def _():
            send_right(k).start()

        for j in range(D2 // TILE):
            cols = slice(j * TILE, (j + 1) * TILE)
            acc[:, cols] = dot_nt(rk[1, k * ROWS : (k + 1) * ROWS], wd[cols])
        for i in range(8):
            low, high = low_high(k, i)
            rows = pl.ds(i * CH, CH)
            xs[low] = (xs[low].astype(F32) + acc[rows, :D]).astype(BF)
            xs[high] = (xs[high].astype(F32) + acc[rows, D:]).astype(BF)

    mix_copies = []
    for r, dev, target in group:
        mix_copies.append(remote(xs.at[target], mixed.at[own_rows], mix_s.at[r], mix_r.at[r], dev))
    own_mix = pltpu.make_async_copy(xs.at[me], mixed.at[own_rows], loc.at[2])
    own_mix.start()
    for copy in mix_copies:
        copy.start()

    own_cot.wait()
    for copy in cot_copies:
        copy.wait()

    for k in (3, 2, 1, 0):
        for i in range(8):
            low, high = low_high(k, i)
            rows = pl.ds(i * CH, CH)
            gpv[rows, :D] = gs[low]
            gpv[rows, D:] = gs[high]
        lk[1, :, k * ROWS : (k + 1) * ROWS] = gpv[...].T

        @pl.when(c == 0)
        def _():
            send_left(k).start()

        for j in range(FF // TILE):
            cols = slice(j * TILE, (j + 1) * TILE)
            d_hidden = dot_nn(gpv[...], wd[:, cols])
            rk[0, k * ROWS : (k + 1) * ROWS, cols] = (d_hidden * slope[k, :, cols]).astype(BF)

        @pl.when(c == 1)
        def _():
            send_right(k).start()

        if k > 0:
            for j in range(D2 // TILE):
                cols = slice(j * TILE, (j + 1) * TILE)
                acc[:, cols] = dot_nt(rk[0, k * ROWS : (k + 1) * ROWS], wu[cols])
            for i in range(8):
                low, high = low_high(k, i)
                rows = pl.ds(i * CH, CH)
                d_norm = acc[rows]
                normed = nf[k, rows]
                first = jnp.mean(d_norm, axis=-1, keepdims=True)
                second = jnp.mean(d_norm * normed, axis=-1, keepdims=True)
                d_pair = rs[k, rows] * (d_norm - first - normed * second)
                gs[low] = (gs[low].astype(F32) + d_pair[:, :D]).astype(BF)
                gs[high] = (gs[high].astype(F32) + d_pair[:, D:]).astype(BF)

    for k in range(4):
        send_left(k).wait()
        send_right(k).wait()

    count = [0]

    def link(src, dst, dev):
        n = count[0]
        count[0] += 1
        return remote(src, dst, red_s.at[n], red_r.at[n], dev)

    def mrow(group_y, half):
        return pl.ds(pl.multiple_of(group_y * 192 + half * 96, 48), 96)

    def hrow(group_y, part):
        return pl.ds(pl.multiple_of(group_y * 192 + part * 48, 48), 48)

    a1 = [[link(sa1.at[i, d], ra1.at[i, d], ydev[d]) for d in range(2)] for i in range(4)]
    a2 = [[link(sa2.at[i, d], ra2.at[i, d], ydev[d]) for d in range(2)] for i in range(4)]
    x1 = [link(sx1.at[d], rx1.at[d], xdev[d]) for d in range(2)]
    x2 = [link(sx2.at[d], rx2.at[d], xdev[d]) for d in range(2)]
    b1 = [link(sb1.at[d], rb1.at[d], xdev[d]) for d in range(2)]
    b2 = [link(sb2.at[d], rb2.at[d], xdev[d]) for d in range(2)]
    y1c = [link(sy1.at[d], ry1.at[d], ydev[d]) for d in range(2)]
    y2c = [link(sy2.at[d], ry2.at[d], ydev[d]) for d in range(2)]

    def unit(i):
        xt = (x + (2, 1, 3, 0)[i]) % 4
        cols = pl.ds(pl.multiple_of(xt * 384, 128), 384)

        def body(t, carry):
            rows = pl.ds(pl.multiple_of(t * 256, 256), 256)
            m4[i, rows] = dot_nn(lk[c, rows], rk[c, :, cols])
            return carry

        lax.fori_loop(0, 3, body, 0)

    def a_first(i):
        for d in range(2):
            sa1[i, d] = m4[i, hrow(y2, d)].astype(BF)
            a1[i][d].start()

    def a_second(i):
        for d, target in enumerate((yp, ym)):
            a1[i][d].wait()
            lo, hi = m4[i, hrow(target, 0)], m4[i, hrow(target, 1)]
            if d == 0:
                lo = lo + ra1[i, d].astype(F32)
            else:
                hi = hi + ra1[i, d].astype(F32)
            sa2[i, d, :48] = lo.astype(BF)
            sa2[i, d, 48:] = hi.astype(BF)
            a2[i][d].start()

    def a_final(i):
        for d in range(2):
            a2[i][d].wait()
        ay[i] = m4[i, mrow(y, 0)] + ra2[i, 0].astype(F32) + ra2[i, 1].astype(F32)

    def b_first():
        for d in range(2):
            for g in range(2):
                sb1[d, g] = m4[0, mrow(2 * d + g, 1)].astype(BF)
            b1[d].start()

    def b_second(d):
        b1[d].wait()
        for g in range(4):
            value = m4[1 + d, mrow(g, 1)]
            if g // 2 == d:
                value = value + rb1[d, g % 2].astype(F32)
            sb2[d, g] = value.astype(BF)
        b2[d].start()

    unit(0)
    a_first(0)
    b_first()
    unit(1)
    a_first(1)
    b_second(0)
    a_second(0)
    unit(2)
    a_first(2)
    b_second(1)
    a_second(1)
    unit(3)
    a_first(3)
    a_second(2)
    a_final(0)
    for d in range(2):
        sx1[d] = ay[0, d * 48 : (d + 1) * 48].astype(BF)
        x1[d].start()
    a_second(3)
    for d in range(2):
        b2[d].wait()
    for g in range(4):
        bx[g] = m4[3, mrow(g, 1)] + rb2[0, g].astype(F32) + rb2[1, g].astype(F32)
    for d in range(2):
        sy1[d] = bx[y2, d * 48 : (d + 1) * 48].astype(BF)
        y1c[d].start()
    for d in range(2):
        a_final(1 + d)
        x1[d].wait()
        rows = slice(d * 48, (d + 1) * 48)
        ay[1 + d, rows] = ay[1 + d, rows] + rx1[d].astype(F32)
        sx2[d] = ay[1 + d].astype(BF)
        x2[d].start()
    for d, target in enumerate((yp, ym)):
        y1c[d].wait()
        rows = slice(d * 48, (d + 1) * 48)
        bx[target, rows] = bx[target, rows] + ry1[d].astype(F32)
        sy2[d] = bx[target].astype(BF)
        y2c[d].start()
    a_final(3)
    for d in range(2):
        x2[d].wait()
    ft[:96] = ay[3] + rx2[0].astype(F32) + rx2[1].astype(F32)
    for d in range(2):
        y2c[d].wait()
    ft[96:] = bx[y] + ry2[0].astype(F32) + ry2[1].astype(F32)
    fz[...] = ft[...].astype(BF)

    z_copies = []
    for d in range(1, 8):
        zd = (z + d) % 8
        rows = pl.ds(pl.multiple_of((zd // 2) * 48, 48), 48)
        cols = pl.ds(pl.multiple_of((zd % 2) * 128, 128), 256)
        z_copies.append(link(fz.at[rows, cols], zr.at[d - 1], zdev[d - 1]))
    for copy in z_copies:
        copy.start()
    rows = pl.ds(pl.multiple_of(zh * 48, 48), 48)
    cols = pl.ds(pl.multiple_of(zl * 128, 128), 256)
    total = ft[rows, cols]
    for d in range(7):
        z_copies[d].wait()
        total = total + zr[d].astype(F32)
    tt[...] = total
    last = link(tt, pt, other)
    last.start()
    gout[c] = total
    last.wait()
    gout[1 - c] = pt[...]

    own_mix.wait()
    for copy in mix_copies:
        copy.wait()


def local(signal, w_up, w_down, cotangent):
    vm = pltpu.VMEM
    dma = pltpu.SemaphoreType.DMA
    anyspec = pl.BlockSpec(memory_space=pl.ANY)
    mixed, grads = pl.pallas_call(
        kernel,
        out_shape=(
            jax.ShapeDtypeStruct((512, D), BF),
            jax.ShapeDtypeStruct((2, 48, 256), F32),
        ),
        in_specs=[anyspec] * 4,
        out_specs=(anyspec, pl.BlockSpec(memory_space=pltpu.VMEM)),
        scratch_shapes=[
            vm((16, CH, D), BF), vm((16, CH, D), BF), vm((ROWS, D2), BF), vm((ROWS, D2), BF),
            vm((4, ROWS, D2), F32), vm((4, ROWS, 1), F32), vm((4, ROWS, FF), F32),
            vm((D2, FF), BF), vm((D2, FF), BF), vm((ROWS, D2), F32),
            vm((2, D2, 8 * ROWS), BF), vm((2, 8 * ROWS, FF), BF),
            vm((4, D2, D), F32), vm((4, 96, D), F32), vm((4, 96, D), F32),
            vm((192, D), BF), vm((192, D), F32),
            vm((4, 2, 48, D), BF), vm((4, 2, 48, D), BF),
            vm((4, 2, 96, D), BF), vm((4, 2, 96, D), BF),
            vm((2, 48, D), BF), vm((2, 48, D), BF), vm((2, 96, D), BF), vm((2, 96, D), BF),
            vm((2, 2, 96, D), BF), vm((2, 2, 96, D), BF),
            vm((2, 4, 96, D), BF), vm((2, 4, 96, D), BF),
            vm((2, 48, D), BF), vm((2, 48, D), BF), vm((2, 96, D), BF), vm((2, 96, D), BF),
            vm((7, 48, 256), BF), vm((48, 256), F32), vm((48, 256), F32),
            dma((16,)), dma((16,)), dma((16,)), dma((16,)), dma((16,)), dma((16,)),
            dma((4,)), dma((4,)), dma((4,)), dma((4,)), dma((4,)),
            dma((40,)), dma((40,)),
        ],
        compiler_params=pltpu.CompilerParams(
            collective_id=0, has_side_effects=True, vmem_limit_bytes=62 << 20
        ),
    )(signal, cotangent, w_up, w_down)
    gy = lax.axis_index("gy")
    start = (gy // 2) % 2 * 64 + gy % 2 * 96
    blocks = lax.dynamic_slice(grads, (0, 0, start), (2, 48, 96))
    return (mixed, blocks[0], blocks[1])


def solution(mesh):
    return jax.shard_map(
        local,
        mesh=mesh,
        in_specs=(P(("gx", "gy"), None), P(), P(), P(("gx", "gy"), None)),
        out_specs=(P(("gx", "gy"), None), P("gx", "gy"), P("gx", "gy")),
        check_vma=False,
    )
```

time: 466 us -> 85.8 us (0.18)
  waiting for transfers between devices: 353 us -> 0 us
  Pallas kernels: 0 us -> 81.6 us
  matrix products: 42.2 us -> 0 us
  starting transfers between devices: 33.6 us -> 0 us
  between operations: 14.4 us -> 0.68 us
  other arithmetic: 10.5 us -> 0 us
  local copies, waits for them, and re-layouts: 9.61 us -> 3.31 us
    reduce_scatter x2 -> x0, waiting for transfers between devices: 170 us -> none  [the longest x1 85.9 us: local(): lax.psum_scatter(total_up.astype(jnp.bfloat16), 'gx', scatter_dimension=0...]
    unnamed x6 -> x0, waiting for transfers between devices: 123 us -> none
    pallas_call x0 -> x1, Pallas kernels: none -> 81.6 us  [local(): pl.pallas_call(kernel, out_shape=(jax.ShapeDtypeStruct((512, D), BF), jax...]
    ppermute x15 -> x0, waiting for transfers between devices: 60.3 us -> none  [swapped(): return lax.ppermute(value, axis, pairs)]
    dot_general x22 -> x0, matrix products: 42.2 us -> none  [the longest x8 24.5 us: contract_first(): lax.dot_general(left, right, (((0,), (0,)), ((), ())), preferred_element_...]
    ppermute x15 -> x0, starting transfers between devices: 33.5 us -> none  [swapped(): return lax.ppermute(value, axis, pairs)]
    unnamed x76 -> x1, local copies, waits for them, and re-layouts: 9.61 us -> 1.78 us
    select_n x22 -> x0, other arithmetic: 6.19 us -> none  [the longest x7 3.69 us: return_halves(): jnp.where(lower, jnp.concatenate([mine, returned], 0), jnp.concatenate([r...]
  transfers between devices with their start and end apart: 19 -> 0, of which waited for: 17 -> 0; matrix products, arithmetic and copies ran while one was open for 6% -> 0% of each run, Pallas kernels for 0% -> 0%
where the time goes in v1:
time: 85.8 us; the launch traced here: 85.6 us
  Pallas kernels  81.6 us (95%)
  local copies, waits for them, and re-layouts  3.31 us (4%)
    pallas_call x1, Pallas kernels, local(): pl.pallas_call(kernel, out_shape=(jax.ShapeDtypeStruct((512, D), BF), jax...  81.6 us
    unnamed x1, local copies, waits for them, and re-layouts  1.78 us

profile of v1, /device:TPU:1, one launch (start us, length us, event | category | flops | bytes accessed | tf_op | source)
XLA Modules:
  0.0 85.6 jit_solution(11624253625323560437)
XLA Ops:
  0.7 81.6 %shard_map.67 = (bf16[512,384]{1,0:T(8,128)(2,1)}, f32[2,48,256]{2,1,0:T(8,128)}) custom-call(bf16[512,384]{1,0:T(8,128)(2,1)} %sig.1, bf16[512,384]{1,0:T(8,128)(2,1)} %cot.1, bf16[768,1536]{1,0:T(8,128)(2,1)} %wu_hbm.1, bf16[768,1536]{1,0:T(8,128)(2,1)} %wd_hbm.1), custom_call_target="tpu_custom_call" | custom-call | tf_op jit(solution)/shard_map/pallas_call | solution.py:352
  82.3 1.5 %dynamic-slice_bitcast_fusion = (f32[48,96]{1,0:T(8,128)}, f32[48,96]{1,0:T(8,128)}) fusion(f32[2,48,256]{2,1,0:T(8,128)} %get-tuple-element.6, s32[]{:T(128)S(6)} %add.18, s32[]{:T(128)S(6)} %select_n.21), kind=kLoop, calls=%fused_computation | loop fusion | bytes 73736 | tf_op jit(solution)/shard_map/squeeze | solution.py:385
  83.8 1.8 %copy.8 = bf16[512,384]{1,0:T(8,128)(2,1)} copy(bf16[512,384]{1,0:T(8,128)(2,1)} %get-tuple-element.12) | data formatting | bytes 786432

commit v2 on v1

--- a/solution.py
+++ b/solution.py
@@ -28,7 +28,7 @@
 
 def kernel(
     sig, cot, wu_hbm, wd_hbm, mixed, gout,
-    xs, gs, nbv, gpv, nf, rs, slope, wu, wd, acc, lk, rk, m4, ay, bx, fz, ft,
+    xs, gs, nbv, gpv, nf, rs, slope, prev, wu, wd, acc, lk, rk, m4, ay, bx, fz, ft,
     sa1, ra1, sa2, ra2, sx1, rx1, sx2, rx2, sb1, rb1, sb2, rb2, sy1, ry1, sy2, ry2, zr, pt, tt,
     sig_s, sig_r, cot_s, cot_r, mix_s, mix_r, loc, lk_s, lk_r, rk_s, rk_r, red_s, red_r,
 ):
@@ -87,13 +87,13 @@
         cot_copies.append(remote(cot.at[rows], gs.at[me], cot_s.at[r], cot_r.at[r], dev))
     for copy in sig_copies:
         copy.start()
-    for copy in cot_copies:
-        copy.start()
     load_wu.wait()
     load_wd.wait()
     own_sig.wait()
     for copy in sig_copies:
         copy.wait()
+    for copy in cot_copies:
+        copy.start()
 
     def low_high(k, i):
         stride = 8 >> k
@@ -123,31 +123,41 @@
             nf[k, rows] = normed
             rs[k, rows] = factor
             nbv[rows] = normed.astype(BF)
-        lk[0, :, k * ROWS : (k + 1) * ROWS] = nbv[...].T
+        mine = slice(k * ROWS, (k + 1) * ROWS)
+        for j in range(FF // TILE):
+            cols = slice(j * TILE, (j + 1) * TILE)
+            pre = dot_nn(nbv[...], wu[:, cols])
+            half = 0.5 + 0.5 * lax.erf(pre * (1.0 / math.sqrt(2.0)))
+            rk[1, mine, cols] = (pre * half).astype(BF)
+            prev[:, cols] = pre
+            slope[k, :, cols] = half
+            if j % 2 == 1:
+                part = slice(j // 2 * TILE, (j // 2 + 1) * TILE)
+                lk[0, part, mine] = nbv[:, part].T
+        for j in range(D2 // TILE):
+            cols = slice(j * TILE, (j + 1) * TILE)
+            out = dot_nt(rk[1, mine], wd[cols])
+            for i in range(8):
+                low, high = low_high(k, i)
+                for at_pos, first in ((low, 0), (high, D)):
+                    lo, hi = max(first, j * TILE), min(first + D, (j + 1) * TILE)
+                    if lo < hi:
+                        here = slice(lo - first, hi - first)
+                        value = out[i * CH : (i + 1) * CH, lo - j * TILE : hi - j * TILE]
+                        xs[at_pos, :, here] = (xs[at_pos, :, here].astype(F32) + value).astype(BF)
+            for t in (2 * j, 2 * j + 1):
+                cols = slice(t * TILE, (t + 1) * TILE)
+                pre = prev[:, cols]
+                bell = jnp.exp2(pre * pre * (-0.5 * math.log2(math.e)))
+                slope[k, :, cols] = slope[k, :, cols] + pre * (1.0 / math.sqrt(2.0 * math.pi)) * bell
 
         @pl.when(c == 1)
         def _():
             send_left(k).start()
 
-        for j in range(FF // TILE):
-            cols = slice(j * TILE, (j + 1) * TILE)
-            pre = dot_nn(nbv[...], wu[:, cols])
-            half = 0.5 * (1.0 + lax.erf(pre * (1.0 / math.sqrt(2.0))))
-            rk[1, k * ROWS : (k + 1) * ROWS, cols] = (pre * half).astype(BF)
-            slope[k, :, cols] = half + pre * jnp.exp(-0.5 * pre * pre) * (1.0 / math.sqrt(2.0 * math.pi))
-
         @pl.when(c == 0)
         def _():
             send_right(k).start()
-
-        for j in range(D2 // TILE):
-            cols = slice(j * TILE, (j + 1) * TILE)
-            acc[:, cols] = dot_nt(rk[1, k * ROWS : (k + 1) * ROWS], wd[cols])
-        for i in range(8):
-            low, high = low_high(k, i)
-            rows = pl.ds(i * CH, CH)
-            xs[low] = (xs[low].astype(F32) + acc[rows, :D]).astype(BF)
-            xs[high] = (xs[high].astype(F32) + acc[rows, D:]).astype(BF)
 
     mix_copies = []
     for r, dev, target in group:
@@ -167,16 +177,18 @@
             rows = pl.ds(i * CH, CH)
             gpv[rows, :D] = gs[low]
             gpv[rows, D:] = gs[high]
-        lk[1, :, k * ROWS : (k + 1) * ROWS] = gpv[...].T
+        mine = slice(k * ROWS, (k + 1) * ROWS)
+        for j in range(FF // TILE):
+            cols = slice(j * TILE, (j + 1) * TILE)
+            d_hidden = dot_nn(gpv[...], wd[:, cols])
+            rk[0, mine, cols] = (d_hidden * slope[k, :, cols]).astype(BF)
+            if j < 3:
+                part = slice(j * TILE, (j + 1) * TILE)
+                lk[1, part, mine] = gpv[:, part].T
 
         @pl.when(c == 0)
         def _():
             send_left(k).start()
-
-        for j in range(FF // TILE):
-            cols = slice(j * TILE, (j + 1) * TILE)
-            d_hidden = dot_nn(gpv[...], wd[:, cols])
-            rk[0, k * ROWS : (k + 1) * ROWS, cols] = (d_hidden * slope[k, :, cols]).astype(BF)
 
         @pl.when(c == 1)
         def _():
@@ -214,124 +226,168 @@
     def hrow(group_y, part):
         return pl.ds(pl.multiple_of(group_y * 192 + part * 48, 48), 48)
 
+    def span(first, size=48):
+        return pl.ds(first * 48, size)
+
     a1 = [[link(sa1.at[i, d], ra1.at[i, d], ydev[d]) for d in range(2)] for i in range(4)]
-    a2 = [[link(sa2.at[i, d], ra2.at[i, d], ydev[d]) for d in range(2)] for i in range(4)]
+    a2 = [
+        [[link(sa2.at[i, d, span(h)], ra2.at[i, d, span(h)], ydev[d]) for h in range(2)] for d in range(2)]
+        for i in range(4)
+    ]
     x1 = [link(sx1.at[d], rx1.at[d], xdev[d]) for d in range(2)]
-    x2 = [link(sx2.at[d], rx2.at[d], xdev[d]) for d in range(2)]
-    b1 = [link(sb1.at[d], rb1.at[d], xdev[d]) for d in range(2)]
-    b2 = [link(sb2.at[d], rb2.at[d], xdev[d]) for d in range(2)]
+    x2 = [[link(sx2.at[d, span(h)], rx2.at[d, span(h)], xdev[d]) for h in range(2)] for d in range(2)]
+    b1 = [[link(sb1.at[d, g], rb1.at[d, g], xdev[d]) for g in range(2)] for d in range(2)]
+    b2 = [[link(sb2.at[d, g], rb2.at[d, g], xdev[d]) for g in range(4)] for d in range(2)]
     y1c = [link(sy1.at[d], ry1.at[d], ydev[d]) for d in range(2)]
-    y2c = [link(sy2.at[d], ry2.at[d], ydev[d]) for d in range(2)]
-
-    def unit(i):
+    y2c = [[link(sy2.at[d, span(h)], ry2.at[d, span(h)], ydev[d]) for h in range(2)] for d in range(2)]
+    near = (yp, ym)
+
+    def unit_cols(i, first, size):
         xt = (x + (2, 1, 3, 0)[i]) % 4
-        cols = pl.ds(pl.multiple_of(xt * 384, 128), 384)
-
+        return pl.ds(pl.multiple_of(xt * 384 + first, 128), size)
+
+    def wide(i):
         def body(t, carry):
             rows = pl.ds(pl.multiple_of(t * 256, 256), 256)
-            m4[i, rows] = dot_nn(lk[c, rows], rk[c, :, cols])
+            m4[i, rows, :256] = dot_nn(lk[c, rows], rk[c, :, unit_cols(i, 0, 256)])
             return carry
 
         lax.fori_loop(0, 3, body, 0)
 
-    def a_first(i):
+    def shared(i):
+        def body(t, carry):
+            rows = pl.ds(pl.multiple_of(t * 256, 256), 256)
+            right = jnp.concatenate(
+                [rk[c, :, unit_cols(i, 256, 128)], rk[c, :, unit_cols(i + 1, 256, 128)]], axis=1
+            )
+            out = dot_nn(lk[c, rows], right)
+            m4[i, rows, 256:] = out[:, :128]
+            m4[i + 1, rows, 256:] = out[:, 128:]
+            return carry
+
+        lax.fori_loop(0, 3, body, 0)
+
+    def a_open(i):
         for d in range(2):
             sa1[i, d] = m4[i, hrow(y2, d)].astype(BF)
             a1[i][d].start()
-
-    def a_second(i):
-        for d, target in enumerate((yp, ym)):
+        for d in range(2):
+            sa2[i, d, (1 - d) * 48 : (2 - d) * 48] = m4[i, hrow(near[d], 1 - d)].astype(BF)
+            a2[i][d][1 - d].start()
+
+    def a_pass(i):
+        for d in range(2):
             a1[i][d].wait()
-            lo, hi = m4[i, hrow(target, 0)], m4[i, hrow(target, 1)]
-            if d == 0:
-                lo = lo + ra1[i, d].astype(F32)
-            else:
-                hi = hi + ra1[i, d].astype(F32)
-            sa2[i, d, :48] = lo.astype(BF)
-            sa2[i, d, 48:] = hi.astype(BF)
-            a2[i][d].start()
+            sa2[i, d, d * 48 : (d + 1) * 48] = (m4[i, hrow(near[d], d)] + ra1[i, d].astype(F32)).astype(BF)
+            a2[i][d][d].start()
 
     def a_final(i):
         for d in range(2):
-            a2[i][d].wait()
+            a2[i][d][1 - d].wait()
+            a2[i][d][d].wait()
         ay[i] = m4[i, mrow(y, 0)] + ra2[i, 0].astype(F32) + ra2[i, 1].astype(F32)
 
-    def b_first():
-        for d in range(2):
-            for g in range(2):
+    def b_open():
+        for g in range(2):
+            for d in range(2):
                 sb1[d, g] = m4[0, mrow(2 * d + g, 1)].astype(BF)
-            b1[d].start()
-
-    def b_second(d):
-        b1[d].wait()
-        for g in range(4):
-            value = m4[1 + d, mrow(g, 1)]
-            if g // 2 == d:
-                value = value + rb1[d, g % 2].astype(F32)
-            sb2[d, g] = value.astype(BF)
-        b2[d].start()
-
-    unit(0)
-    a_first(0)
-    b_first()
-    unit(1)
-    a_first(1)
-    b_second(0)
-    a_second(0)
-    unit(2)
-    a_first(2)
-    b_second(1)
-    a_second(1)
-    unit(3)
-    a_first(3)
-    a_second(2)
+                b1[d][g].start()
+
+    def b_free(d):
+        for g in (2 - 2 * d, 3 - 2 * d):
+            sb2[d, g] = m4[1 + d, mrow(g, 1)].astype(BF)
+            b2[d][g].start()
+
+    def b_pass(d):
+        for h in range(2):
+            g = 2 * d + h
+            b1[d][h].wait()
+            sb2[d, g] = (m4[1 + d, mrow(g, 1)] + rb1[d, h].astype(F32)).astype(BF)
+            b2[d][g].start()
+
+    wide(0)
+    shared(0)
+    b_open()
+    a_open(0)
+    wide(1)
+    b_free(0)
+    a_open(1)
+    wide(2)
+    a_pass(0)
+    shared(2)
+    b_free(1)
+    a_open(2)
+    b_pass(0)
+    b_pass(1)
+    wide(3)
+    a_open(3)
+    a_pass(1)
+    a_pass(2)
     a_final(0)
     for d in range(2):
         sx1[d] = ay[0, d * 48 : (d + 1) * 48].astype(BF)
         x1[d].start()
-    a_second(3)
-    for d in range(2):
-        b2[d].wait()
+    a_pass(3)
+    for d in range(2):
+        a_final(1 + d)
+        free = slice((1 - d) * 48, (2 - d) * 48)
+        sx2[d, free] = ay[1 + d, free].astype(BF)
+        x2[d][1 - d].start()
+    for d in range(2):
+        for g in range(4):
+            b2[d][g].wait()
     for g in range(4):
         bx[g] = m4[3, mrow(g, 1)] + rb2[0, g].astype(F32) + rb2[1, g].astype(F32)
     for d in range(2):
         sy1[d] = bx[y2, d * 48 : (d + 1) * 48].astype(BF)
         y1c[d].start()
     for d in range(2):
-        a_final(1 + d)
+        free = slice((1 - d) * 48, (2 - d) * 48)
+        sy2[d, free] = bx[near[d], free].astype(BF)
+        y2c[d][1 - d].start()
+    for d in range(2):
         x1[d].wait()
-        rows = slice(d * 48, (d + 1) * 48)
-        ay[1 + d, rows] = ay[1 + d, rows] + rx1[d].astype(F32)
-        sx2[d] = ay[1 + d].astype(BF)
-        x2[d].start()
-    for d, target in enumerate((yp, ym)):
+        held = slice(d * 48, (d + 1) * 48)
+        sx2[d, held] = (ay[1 + d, held] + rx1[d].astype(F32)).astype(BF)
+        x2[d][d].start()
+    a_final(3)
+    for d in range(2):
         y1c[d].wait()
-        rows = slice(d * 48, (d + 1) * 48)
-        bx[target, rows] = bx[target, rows] + ry1[d].astype(F32)
-        sy2[d] = bx[target].astype(BF)
-        y2c[d].start()
-    a_final(3)
-    for d in range(2):
-        x2[d].wait()
-    ft[:96] = ay[3] + rx2[0].astype(F32) + rx2[1].astype(F32)
-    for d in range(2):
-        y2c[d].wait()
-    ft[96:] = bx[y] + ry2[0].astype(F32) + ry2[1].astype(F32)
-    fz[...] = ft[...].astype(BF)
+        held = slice(d * 48, (d + 1) * 48)
+        sy2[d, held] = (bx[near[d], held] + ry1[d].astype(F32)).astype(BF)
+        y2c[d][d].start()
 
     z_copies = []
     for d in range(1, 8):
         zd = (z + d) % 8
         rows = pl.ds(pl.multiple_of((zd // 2) * 48, 48), 48)
         cols = pl.ds(pl.multiple_of((zd % 2) * 128, 128), 256)
-        z_copies.append(link(fz.at[rows, cols], zr.at[d - 1], zdev[d - 1]))
-    for copy in z_copies:
-        copy.start()
+        z_copies.append((zd, link(fz.at[rows, cols], zr.at[d - 1], zdev[d - 1])))
+
+    def z_send(part):
+        for zd, copy in z_copies:
+
+            @pl.when(zd // 4 == part)
+            def _():
+                copy.start()
+
+    for d in range(2):
+        x2[d][1 - d].wait()
+        x2[d][d].wait()
+    ft[:96] = ay[3] + rx2[0].astype(F32) + rx2[1].astype(F32)
+    fz[:96] = ft[:96].astype(BF)
+    z_send(0)
+    for d in range(2):
+        y2c[d][1 - d].wait()
+        y2c[d][d].wait()
+    ft[96:] = bx[y] + ry2[0].astype(F32) + ry2[1].astype(F32)
+    fz[96:] = ft[96:].astype(BF)
+    z_send(1)
     rows = pl.ds(pl.multiple_of(zh * 48, 48), 48)
     cols = pl.ds(pl.multiple_of(zl * 128, 128), 256)
     total = ft[rows, cols]
     for d in range(7):
-        z_copies[d].wait()
+        z_copies[d][1].wait()
         total = total + zr[d].astype(F32)
     tt[...] = total
     last = link(tt, pt, other)
@@ -343,6 +399,14 @@
     own_mix.wait()
     for copy in mix_copies:
         copy.wait()
+
+
+def finish(mixed, grads, mixed_out, up_out, down_out):
+    gy = lax.axis_index("gy")
+    start = (gy // 2) % 2 * 64 + gy % 2 * 96
+    mixed_out[...] = mixed[...]
+    for i, out in enumerate((up_out, down_out)):
+        out[...] = pltpu.roll(grads[i], (256 - start) % 256, 1)[:, :96]
 
 
 def local(signal, w_up, w_down, cotangent):
@@ -359,7 +423,7 @@
         out_specs=(anyspec, pl.BlockSpec(memory_space=pltpu.VMEM)),
         scratch_shapes=[
             vm((16, CH, D), BF), vm((16, CH, D), BF), vm((ROWS, D2), BF), vm((ROWS, D2), BF),
-            vm((4, ROWS, D2), F32), vm((4, ROWS, 1), F32), vm((4, ROWS, FF), F32),
+            vm((4, ROWS, D2), F32), vm((4, ROWS, 1), F32), vm((4, ROWS, FF), F32), vm((ROWS, FF), F32),
             vm((D2, FF), BF), vm((D2, FF), BF), vm((ROWS, D2), F32),
             vm((2, D2, 8 * ROWS), BF), vm((2, 8 * ROWS, FF), BF),
             vm((4, D2, D), F32), vm((4, 96, D), F32), vm((4, 96, D), F32),
@@ -373,16 +437,22 @@
             vm((7, 48, 256), BF), vm((48, 256), F32), vm((48, 256), F32),
             dma((16,)), dma((16,)), dma((16,)), dma((16,)), dma((16,)), dma((16,)),
             dma((4,)), dma((4,)), dma((4,)), dma((4,)), dma((4,)),
-            dma((40,)), dma((40,)),
+            dma((64,)), dma((64,)),
         ],
         compiler_params=pltpu.CompilerParams(
             collective_id=0, has_side_effects=True, vmem_limit_bytes=62 << 20
         ),
     )(signal, cotangent, w_up, w_down)
-    gy = lax.axis_index("gy")
-    start = (gy // 2) % 2 * 64 + gy % 2 * 96
-    blocks = lax.dynamic_slice(grads, (0, 0, start), (2, 48, 96))
-    return (mixed, blocks[0], blocks[1])
+    return pl.pallas_call(
+        finish,
+        out_shape=(
+            jax.ShapeDtypeStruct((512, D), BF),
+            jax.ShapeDtypeStruct((48, 96), F32),
+            jax.ShapeDtypeStruct((48, 96), F32),
+        ),
+        in_specs=[pl.BlockSpec(memory_space=pltpu.VMEM)] * 2,
+        out_specs=(pl.BlockSpec(memory_space=pltpu.VMEM),) * 3,
+    )(mixed, grads)
 
 
 def solution(mesh):

time: 85.8 us -> 73.6 us (0.86)
  Pallas kernels: 81.6 us -> 72.8 us
  local copies, waits for them, and re-layouts: 3.31 us -> 0 us
    pallas_call x1, Pallas kernels: 81.6 us -> 71 us  [local(): pl.pallas_call(kernel, out_shape=(jax.ShapeDtypeStruct((512, D), BF), jax...]
    pallas_call x0 -> x1, Pallas kernels: none -> 1.81 us  [local(): pl.pallas_call(finish, out_shape=(jax.ShapeDtypeStruct((512, D), BF), jax...]
    unnamed x1 -> x0, local copies, waits for them, and re-layouts: 1.78 us -> none
    squeeze x1 -> x0, local copies, waits for them, and re-layouts: 1.53 us -> none  [local(): return (mixed, blocks[0], blocks[1])]
where the time goes in v2:
time: 73.6 us; the launch traced here: 73.5 us
  Pallas kernels  72.8 us (99%)
    pallas_call x1, Pallas kernels, local(): pl.pallas_call(kernel, out_shape=(jax.ShapeDtypeStruct((512, D), BF), jax...  71 us
    pallas_call x1, Pallas kernels, local(): pl.pallas_call(finish, out_shape=(jax.ShapeDtypeStruct((512, D), BF), jax...  1.81 us

profile of v2, /device:TPU:1, one launch (start us, length us, event | category | flops | bytes accessed | tf_op | source)
XLA Modules:
  0.0 73.5 jit_solution(8264940319437157007)
XLA Ops:
  0.6 71.0 %shard_map.67 = (bf16[512,384]{1,0:T(8,128)(2,1)}, f32[2,48,256]{2,1,0:T(8,128)}) custom-call(bf16[512,384]{1,0:T(8,128)(2,1)} %sig.1, bf16[512,384]{1,0:T(8,128)(2,1)} %cot.1, bf16[768,1536]{1,0:T(8,128)(2,1)} %wu_hbm.1, bf16[768,1536]{1,0:T(8,128)(2,1)} %wd_hbm.1), custom_call_target="tpu_custom_call" | custom-call | tf_op jit(solution)/shard_map/pallas_call | solution.py:416
  71.7 1.8 %shard_map.68 = (bf16[512,384]{1,0:T(8,128)(2,1)}, f32[48,96]{1,0:T(8,128)}, f32[48,96]{1,0:T(8,128)}) custom-call(bf16[512,384]{1,0:T(8,128)(2,1)} %get-tuple-element.5.mixed, f32[2,48,256]{2,1,0:T(8,128)} %get-tuple-element.6.grads), custom_call_target="tpu_custom_call" | custom-call | tf_op jit(solution)/shard_map/pallas_call | solution.py:446

commit v3 on v2

--- a/solution.py
+++ b/solution.py
@@ -83,17 +83,22 @@
     sig_copies, cot_copies = [], []
     for r, dev, target in reversed(group):
         rows = pl.ds(pl.multiple_of(target * CH, CH), CH)
-        sig_copies.append(remote(sig.at[rows], xs.at[me], sig_s.at[r], sig_r.at[r], dev))
-        cot_copies.append(remote(cot.at[rows], gs.at[me], cot_s.at[r], cot_r.at[r], dev))
+        sig_copies.append(remote(sig.at[rows], xs.at[me], sig_s.at[0], sig_r.at[0], dev))
+        cot_copies.append(remote(cot.at[rows], gs.at[me], cot_s.at[0], cot_r.at[0], dev))
     for copy in sig_copies:
         copy.start()
     load_wu.wait()
     load_wd.wait()
     own_sig.wait()
-    for copy in sig_copies:
-        copy.wait()
+    most = pl.ds(0, 15)
+    wide_rows = pl.ds(0, 15 * CH)
+    all_sig = remote(sig.at[wide_rows], xs.at[most], sig_s.at[0], sig_r.at[0], other)
+    all_cot = remote(cot.at[wide_rows], gs.at[most], cot_s.at[0], cot_r.at[0], other)
+    all_mix = remote(xs.at[most], mixed.at[wide_rows], mix_s.at[0], mix_r.at[0], other)
+    all_sig.wait_send()
     for copy in cot_copies:
         copy.start()
+    all_sig.wait_recv()
 
     def low_high(k, i):
         stride = 8 >> k
@@ -134,6 +139,11 @@
             if j % 2 == 1:
                 part = slice(j // 2 * TILE, (j // 2 + 1) * TILE)
                 lk[0, part, mine] = nbv[:, part].T
+
+        @pl.when(c == 0)
+        def _():
+            send_right(k).start()
+
         for j in range(D2 // TILE):
             cols = slice(j * TILE, (j + 1) * TILE)
             out = dot_nt(rk[1, mine], wd[cols])
@@ -155,21 +165,16 @@
         def _():
             send_left(k).start()
 
-        @pl.when(c == 0)
-        def _():
-            send_right(k).start()
-
     mix_copies = []
     for r, dev, target in group:
-        mix_copies.append(remote(xs.at[target], mixed.at[own_rows], mix_s.at[r], mix_r.at[r], dev))
+        mix_copies.append(remote(xs.at[target], mixed.at[own_rows], mix_s.at[0], mix_r.at[0], dev))
     own_mix = pltpu.make_async_copy(xs.at[me], mixed.at[own_rows], loc.at[2])
     own_mix.start()
     for copy in mix_copies:
         copy.start()
 
     own_cot.wait()
-    for copy in cot_copies:
-        copy.wait()
+    all_cot.wait()
 
     for k in (3, 2, 1, 0):
         for i in range(8):
@@ -236,11 +241,15 @@
     ]
     x1 = [link(sx1.at[d], rx1.at[d], xdev[d]) for d in range(2)]
     x2 = [[link(sx2.at[d, span(h)], rx2.at[d, span(h)], xdev[d]) for h in range(2)] for d in range(2)]
-    b1 = [[link(sb1.at[d, g], rb1.at[d, g], xdev[d]) for g in range(2)] for d in range(2)]
-    b2 = [[link(sb2.at[d, g], rb2.at[d, g], xdev[d]) for g in range(4)] for d in range(2)]
+    b1 = [[link(sb1.at[d, g], rb1.at[d, g], xdev[d]) for g in range(4)] for d in range(2)]
+    b2 = [
+        [[link(sb2.at[d, g, span(h)], rb2.at[d, g, span(h)], xdev[d]) for h in range(2)] for g in range(4)]
+        for d in range(2)
+    ]
     y1c = [link(sy1.at[d], ry1.at[d], ydev[d]) for d in range(2)]
     y2c = [[link(sy2.at[d, span(h)], ry2.at[d, span(h)], ydev[d]) for h in range(2)] for d in range(2)]
     near = (yp, ym)
+    order = (y2, yp, ym, y)
 
     def unit_cols(i, first, size):
         xt = (x + (2, 1, 3, 0)[i]) % 4
@@ -288,74 +297,87 @@
         ay[i] = m4[i, mrow(y, 0)] + ra2[i, 0].astype(F32) + ra2[i, 1].astype(F32)
 
     def b_open():
-        for g in range(2):
+        for g in range(4):
             for d in range(2):
-                sb1[d, g] = m4[0, mrow(2 * d + g, 1)].astype(BF)
+                sb1[d, g] = m4[0, hrow(order[g], 2 + d)].astype(BF)
                 b1[d][g].start()
 
-    def b_free(d):
-        for g in (2 - 2 * d, 3 - 2 * d):
-            sb2[d, g] = m4[1 + d, mrow(g, 1)].astype(BF)
-            b2[d][g].start()
-
-    def b_pass(d):
-        for h in range(2):
-            g = 2 * d + h
-            b1[d][h].wait()
-            sb2[d, g] = (m4[1 + d, mrow(g, 1)] + rb1[d, h].astype(F32)).astype(BF)
-            b2[d][g].start()
+    def b_free(d, g):
+        free = slice((1 - d) * 48, (2 - d) * 48)
+        sb2[d, g, free] = m4[1 + d, hrow(order[g], 3 - d)].astype(BF)
+        b2[d][g][1 - d].start()
+
+    def b_pass(d, g):
+        held = slice(d * 48, (d + 1) * 48)
+        b1[d][g].wait()
+        sb2[d, g, held] = (m4[1 + d, hrow(order[g], 2 + d)] + rb1[d, g].astype(F32)).astype(BF)
+        b2[d][g][d].start()
+
+    def b_final(g):
+        for d in range(2):
+            b2[d][g][1 - d].wait()
+            b2[d][g][d].wait()
+        bx[g] = m4[3, mrow(order[g], 1)] + rb2[0, g].astype(F32) + rb2[1, g].astype(F32)
+
+    def open_last(first, value, staged):
+        for d in range(2):
+            staged[d] = value[0, d * 48 : (d + 1) * 48].astype(BF)
+            first[d].start()
+
+    def pass_last(d, first, second, value, staged, got):
+        free = slice((1 - d) * 48, (2 - d) * 48)
+        held = slice(d * 48, (d + 1) * 48)
+        staged[d, free] = value[1 + d, free].astype(BF)
+        second[d][1 - d].start()
+        first[d].wait()
+        staged[d, held] = (value[1 + d, held] + got[d].astype(F32)).astype(BF)
+        second[d][d].start()
 
     wide(0)
     shared(0)
     b_open()
     a_open(0)
     wide(1)
-    b_free(0)
+    b_free(0, 0)
+    b_free(0, 1)
     a_open(1)
     wide(2)
+    b_pass(0, 0)
+    b_free(0, 2)
+    b_pass(0, 1)
+    b_free(0, 3)
     a_pass(0)
     shared(2)
-    b_free(1)
+    b_free(1, 0)
+    b_pass(1, 0)
+    b_free(1, 1)
+    b_pass(1, 1)
     a_open(2)
-    b_pass(0)
-    b_pass(1)
+    b_pass(0, 2)
+    b_pass(0, 3)
+    b_free(1, 2)
+    b_pass(1, 2)
+    b_free(1, 3)
+    b_pass(1, 3)
+    a_pass(1)
     wide(3)
     a_open(3)
-    a_pass(1)
     a_pass(2)
     a_final(0)
-    for d in range(2):
-        sx1[d] = ay[0, d * 48 : (d + 1) * 48].astype(BF)
-        x1[d].start()
+    open_last(x1, ay, sx1)
+    b_final(0)
+    open_last(y1c, bx, sy1)
+    a_final(1)
+    b_final(1)
     a_pass(3)
-    for d in range(2):
-        a_final(1 + d)
-        free = slice((1 - d) * 48, (2 - d) * 48)
-        sx2[d, free] = ay[1 + d, free].astype(BF)
-        x2[d][1 - d].start()
-    for d in range(2):
-        for g in range(4):
-            b2[d][g].wait()
-    for g in range(4):
-        bx[g] = m4[3, mrow(g, 1)] + rb2[0, g].astype(F32) + rb2[1, g].astype(F32)
-    for d in range(2):
-        sy1[d] = bx[y2, d * 48 : (d + 1) * 48].astype(BF)
-        y1c[d].start()
-    for d in range(2):
-        free = slice((1 - d) * 48, (2 - d) * 48)
-        sy2[d, free] = bx[near[d], free].astype(BF)
-        y2c[d][1 - d].start()
-    for d in range(2):
-        x1[d].wait()
-        held = slice(d * 48, (d + 1) * 48)
-        sx2[d, held] = (ay[1 + d, held] + rx1[d].astype(F32)).astype(BF)
-        x2[d][d].start()
+    pass_last(0, y1c, y2c, bx, sy2, ry1)
+    pass_last(0, x1, x2, ay, sx2, rx1)
+    a_final(2)
+    pass_last(1, x1, x2, ay, sx2, rx1)
+    b_final(2)
+    pass_last(1, y1c, y2c, bx, sy2, ry1)
+    b_final(3)
     a_final(3)
-    for d in range(2):
-        y1c[d].wait()
-        held = slice(d * 48, (d + 1) * 48)
-        sy2[d, held] = (bx[near[d], held] + ry1[d].astype(F32)).astype(BF)
-        y2c[d][d].start()
 
     z_copies = []
     for d in range(1, 8):
@@ -380,7 +402,7 @@
     for d in range(2):
         y2c[d][1 - d].wait()
         y2c[d][d].wait()
-    ft[96:] = bx[y] + ry2[0].astype(F32) + ry2[1].astype(F32)
+    ft[96:] = bx[3] + ry2[0].astype(F32) + ry2[1].astype(F32)
     fz[96:] = ft[96:].astype(BF)
     z_send(1)
     rows = pl.ds(pl.multiple_of(zh * 48, 48), 48)
@@ -397,8 +419,7 @@
     gout[1 - c] = pt[...]
 
     own_mix.wait()
-    for copy in mix_copies:
-        copy.wait()
+    all_mix.wait()
 
 
 def finish(mixed, grads, mixed_out, up_out, down_out):
@@ -431,13 +452,13 @@
             vm((4, 2, 48, D), BF), vm((4, 2, 48, D), BF),
             vm((4, 2, 96, D), BF), vm((4, 2, 96, D), BF),
             vm((2, 48, D), BF), vm((2, 48, D), BF), vm((2, 96, D), BF), vm((2, 96, D), BF),
-            vm((2, 2, 96, D), BF), vm((2, 2, 96, D), BF),
+            vm((2, 4, 48, D), BF), vm((2, 4, 48, D), BF),
             vm((2, 4, 96, D), BF), vm((2, 4, 96, D), BF),
             vm((2, 48, D), BF), vm((2, 48, D), BF), vm((2, 96, D), BF), vm((2, 96, D), BF),
             vm((7, 48, 256), BF), vm((48, 256), F32), vm((48, 256), F32),
-            dma((16,)), dma((16,)), dma((16,)), dma((16,)), dma((16,)), dma((16,)),
+            dma((1,)), dma((1,)), dma((1,)), dma((1,)), dma((1,)), dma((1,)),
             dma((4,)), dma((4,)), dma((4,)), dma((4,)), dma((4,)),
-            dma((64,)), dma((64,)),
+            dma((68,)), dma((68,)),
         ],
         compiler_params=pltpu.CompilerParams(
             collective_id=0, has_side_effects=True, vmem_limit_bytes=62 << 20

time: 73.6 us -> 79.2 us (1.076)
  Pallas kernels: 72.8 us -> 78.4 us
    pallas_call x1, Pallas kernels: 71 us -> 76.6 us  [local(): pl.pallas_call(kernel, out_shape=(jax.ShapeDtypeStruct((512, D), BF), jax...]
where the time goes in v3:
time: 79.2 us; the launch traced here: 79.1 us
  Pallas kernels  78.4 us (99%)
    pallas_call x1, Pallas kernels, local(): pl.pallas_call(kernel, out_shape=(jax.ShapeDtypeStruct((512, D), BF), jax...  76.6 us
    pallas_call x1, Pallas kernels, local(): pl.pallas_call(finish, out_shape=(jax.ShapeDtypeStruct((512, D), BF), jax...  1.81 us

profile of v3, /device:TPU:1, one launch (start us, length us, event | category | flops | bytes accessed | tf_op | source)
XLA Modules:
  0.0 79.1 jit_solution(1122546927091897861)
XLA Ops:
  0.6 76.6 %shard_map.67 = (bf16[512,384]{1,0:T(8,128)(2,1)}, f32[2,48,256]{2,1,0:T(8,128)}) custom-call(bf16[512,384]{1,0:T(8,128)(2,1)} %sig.1, bf16[512,384]{1,0:T(8,128)(2,1)} %cot.1, bf16[768,1536]{1,0:T(8,128)(2,1)} %wu_hbm.1, bf16[768,1536]{1,0:T(8,128)(2,1)} %wd_hbm.1), custom_call_target="tpu_custom_call" | custom-call | tf_op jit(solution)/shard_map/pallas_call | solution.py:437
  77.3 1.8 %shard_map.68 = (bf16[512,384]{1,0:T(8,128)(2,1)}, f32[48,96]{1,0:T(8,128)}, f32[48,96]{1,0:T(8,128)}) custom-call(bf16[512,384]{1,0:T(8,128)(2,1)} %get-tuple-element.5.mixed, f32[2,48,256]{2,1,0:T(8,128)} %get-tuple-element.6.grads), custom_call_target="tpu_custom_call" | custom-call | tf_op jit(solution)/shard_map/pallas_call | solution.py:467

commit v4 on v3

--- a/solution.py
+++ b/solution.py
@@ -95,15 +95,24 @@
     all_sig = remote(sig.at[wide_rows], xs.at[most], sig_s.at[0], sig_r.at[0], other)
     all_cot = remote(cot.at[wide_rows], gs.at[most], cot_s.at[0], cot_r.at[0], other)
     all_mix = remote(xs.at[most], mixed.at[wide_rows], mix_s.at[0], mix_r.at[0], other)
-    all_sig.wait_send()
+    all_sig.wait()
     for copy in cot_copies:
         copy.start()
-    all_sig.wait_recv()
 
     def low_high(k, i):
         stride = 8 >> k
         low = (i // stride) * 2 * stride + i % stride
         return low, low + stride
+
+    def store_turned(which, t, mine, source):
+        turned = source[:, t * TILE : (t + 1) * TILE].T
+        for b in range(TILE // 16):
+            block = t * (TILE // 16) + b
+            group_y, inner = block // 12, block % 12
+            zz, third = inner // 3, inner % 3
+            odd = zz % 2
+            spot = (3 * (zz // 2) + (2 * odd, 1 + 6 * odd, 6 + 2 * odd)[third]) * 16 + group_y * 192
+            lk[which, spot : spot + 16, mine] = turned[b * 16 : (b + 1) * 16]
 
     def send_left(k):
         cols = pl.ds(k * ROWS, ROWS)
@@ -137,8 +146,7 @@
             prev[:, cols] = pre
             slope[k, :, cols] = half
             if j % 2 == 1:
-                part = slice(j // 2 * TILE, (j // 2 + 1) * TILE)
-                lk[0, part, mine] = nbv[:, part].T
+                store_turned(0, j // 2, mine, nbv)
 
         @pl.when(c == 0)
         def _():
@@ -188,8 +196,7 @@
             d_hidden = dot_nn(gpv[...], wd[:, cols])
             rk[0, mine, cols] = (d_hidden * slope[k, :, cols]).astype(BF)
             if j < 3:
-                part = slice(j * TILE, (j + 1) * TILE)
-                lk[1, part, mine] = gpv[:, part].T
+                store_turned(1, j, mine, gpv)
 
         @pl.when(c == 0)
         def _():
@@ -220,9 +227,12 @@
 
     count = [0]
 
-    def link(src, dst, dev):
-        n = count[0]
+    def fresh():
         count[0] += 1
+        return count[0] - 1
+
+    def link(src, dst, dev, n=None):
+        n = fresh() if n is None else n
         return remote(src, dst, red_s.at[n], red_r.at[n], dev)
 
     def mrow(group_y, half):
@@ -235,19 +245,26 @@
         return pl.ds(first * 48, size)
 
     a1 = [[link(sa1.at[i, d], ra1.at[i, d], ydev[d]) for d in range(2)] for i in range(4)]
+    a2n = [fresh() for i in range(4)]
     a2 = [
-        [[link(sa2.at[i, d, span(h)], ra2.at[i, d, span(h)], ydev[d]) for h in range(2)] for d in range(2)]
+        [[link(sa2.at[i, d, span(h)], ra2.at[i, d, span(h)], ydev[d], a2n[i]) for h in range(2)] for d in range(2)]
         for i in range(4)
     ]
+    a2_all = [link(sa2.at[i], ra2.at[i], ydev[0], a2n[i]) for i in range(4)]
     x1 = [link(sx1.at[d], rx1.at[d], xdev[d]) for d in range(2)]
-    x2 = [[link(sx2.at[d, span(h)], rx2.at[d, span(h)], xdev[d]) for h in range(2)] for d in range(2)]
+    x2n, y2n, zn = fresh(), fresh(), fresh()
+    x2 = [[link(sx2.at[d, span(h)], rx2.at[d, span(h)], xdev[d], x2n) for h in range(2)] for d in range(2)]
+    x2_all = link(sx2, rx2, xdev[0], x2n)
     b1 = [[link(sb1.at[d, g], rb1.at[d, g], xdev[d]) for g in range(4)] for d in range(2)]
+    b2n = [fresh() for g in range(4)]
     b2 = [
-        [[link(sb2.at[d, g, span(h)], rb2.at[d, g, span(h)], xdev[d]) for h in range(2)] for g in range(4)]
+        [[link(sb2.at[d, g, span(h)], rb2.at[d, g, span(h)], xdev[d], b2n[g]) for h in range(2)] for g in range(4)]
         for d in range(2)
     ]
+    b2_all = [link(sb2.at[:, g], rb2.at[:, g], xdev[0], b2n[g]) for g in range(4)]
     y1c = [link(sy1.at[d], ry1.at[d], ydev[d]) for d in range(2)]
-    y2c = [[link(sy2.at[d, span(h)], ry2.at[d, span(h)], ydev[d]) for h in range(2)] for d in range(2)]
+    y2c = [[link(sy2.at[d, span(h)], ry2.at[d, span(h)], ydev[d], y2n) for h in range(2)] for d in range(2)]
+    y2_all = link(sy2, ry2, ydev[0], y2n)
     near = (yp, ym)
     order = (y2, yp, ym, y)
 
@@ -256,25 +273,15 @@
         return pl.ds(pl.multiple_of(xt * 384 + first, 128), size)
 
     def wide(i):
-        def body(t, carry):
-            rows = pl.ds(pl.multiple_of(t * 256, 256), 256)
-            m4[i, rows, :256] = dot_nn(lk[c, rows], rk[c, :, unit_cols(i, 0, 256)])
-            return carry
-
-        lax.fori_loop(0, 3, body, 0)
+        m4[i, :, :256] = dot_nn(lk[c], rk[c, :, unit_cols(i, 0, 256)])
 
     def shared(i):
-        def body(t, carry):
-            rows = pl.ds(pl.multiple_of(t * 256, 256), 256)
-            right = jnp.concatenate(
-                [rk[c, :, unit_cols(i, 256, 128)], rk[c, :, unit_cols(i + 1, 256, 128)]], axis=1
-            )
-            out = dot_nn(lk[c, rows], right)
-            m4[i, rows, 256:] = out[:, :128]
-            m4[i + 1, rows, 256:] = out[:, 128:]
-            return carry
-
-        lax.fori_loop(0, 3, body, 0)
+        right = jnp.concatenate(
+            [rk[c, :, unit_cols(i, 256, 128)], rk[c, :, unit_cols(i + 1, 256, 128)]], axis=1
+        )
+        out = dot_nn(lk[c], right)
+        m4[i, :, 256:] = out[:, :128]
+        m4[i + 1, :, 256:] = out[:, 128:]
 
     def a_open(i):
         for d in range(2):
@@ -291,9 +298,7 @@
             a2[i][d][d].start()
 
     def a_final(i):
-        for d in range(2):
-            a2[i][d][1 - d].wait()
-            a2[i][d][d].wait()
+        a2_all[i].wait()
         ay[i] = m4[i, mrow(y, 0)] + ra2[i, 0].astype(F32) + ra2[i, 1].astype(F32)
 
     def b_open():
@@ -314,9 +319,7 @@
         b2[d][g][d].start()
 
     def b_final(g):
-        for d in range(2):
-            b2[d][g][1 - d].wait()
-            b2[d][g][d].wait()
+        b2_all[g].wait()
         bx[g] = m4[3, mrow(order[g], 1)] + rb2[0, g].astype(F32) + rb2[1, g].astype(F32)
 
     def open_last(first, value, staged):
@@ -345,7 +348,6 @@
     b_pass(0, 0)
     b_free(0, 2)
     b_pass(0, 1)
-    b_free(0, 3)
     a_pass(0)
     shared(2)
     b_free(1, 0)
@@ -354,11 +356,8 @@
     b_pass(1, 1)
     a_open(2)
     b_pass(0, 2)
-    b_pass(0, 3)
     b_free(1, 2)
     b_pass(1, 2)
-    b_free(1, 3)
-    b_pass(1, 3)
     a_pass(1)
     wide(3)
     a_open(3)
@@ -368,48 +367,56 @@
     b_final(0)
     open_last(y1c, bx, sy1)
     a_final(1)
+    pass_last(0, x1, x2, ay, sx2, rx1)
+    b_free(0, 3)
+    b_pass(0, 3)
+    a_pass(3)
     b_final(1)
-    a_pass(3)
     pass_last(0, y1c, y2c, bx, sy2, ry1)
-    pass_last(0, x1, x2, ay, sx2, rx1)
     a_final(2)
     pass_last(1, x1, x2, ay, sx2, rx1)
+    b_free(1, 3)
+    b_pass(1, 3)
     b_final(2)
     pass_last(1, y1c, y2c, bx, sy2, ry1)
-    b_final(3)
     a_final(3)
 
+    def third_rows(zz, third):
+        base, odd = (zz // 2) * 48, zz % 2
+        first = (base + odd * 32, base + 16 + odd * 96, base + 96 + odd * 32)[third]
+        return pl.ds(pl.multiple_of(first, 16), 16)
+
     z_copies = []
-    for d in range(1, 8):
+    for d in (4, 3, 5, 2, 6, 1, 7):
         zd = (z + d) % 8
-        rows = pl.ds(pl.multiple_of((zd // 2) * 48, 48), 48)
         cols = pl.ds(pl.multiple_of((zd % 2) * 128, 128), 256)
-        z_copies.append((zd, link(fz.at[rows, cols], zr.at[d - 1], zdev[d - 1])))
+        pieces = [
+            link(fz.at[third_rows(zd // 2, t), cols], zr.at[d - 1, pl.ds(t * 16, 16)], zdev[d - 1], zn)
+            for t in range(3)
+        ]
+        z_copies.append((zd, pieces))
 
     def z_send(part):
-        for zd, copy in z_copies:
-
-            @pl.when(zd // 4 == part)
+        for zd, pieces in z_copies:
+            pieces[2 * part].start()
+
+            @pl.when((zd // 2) % 2 == part)
             def _():
-                copy.start()
-
-    for d in range(2):
-        x2[d][1 - d].wait()
-        x2[d][d].wait()
+                pieces[1].start()
+
+    x2_all.wait()
     ft[:96] = ay[3] + rx2[0].astype(F32) + rx2[1].astype(F32)
     fz[:96] = ft[:96].astype(BF)
     z_send(0)
-    for d in range(2):
-        y2c[d][1 - d].wait()
-        y2c[d][d].wait()
+    b_final(3)
+    y2_all.wait()
     ft[96:] = bx[3] + ry2[0].astype(F32) + ry2[1].astype(F32)
     fz[96:] = ft[96:].astype(BF)
     z_send(1)
-    rows = pl.ds(pl.multiple_of(zh * 48, 48), 48)
     cols = pl.ds(pl.multiple_of(zl * 128, 128), 256)
-    total = ft[rows, cols]
+    total = jnp.concatenate([ft[third_rows(zh, t), cols] for t in range(3)], axis=0)
+    link(zr, zr, zdev[0], zn).wait()
     for d in range(7):
-        z_copies[d][1].wait()
         total = total + zr[d].astype(F32)
     tt[...] = total
     last = link(tt, pt, other)
@@ -458,7 +465,7 @@
             vm((7, 48, 256), BF), vm((48, 256), F32), vm((48, 256), F32),
             dma((1,)), dma((1,)), dma((1,)), dma((1,)), dma((1,)), dma((1,)),
             dma((4,)), dma((4,)), dma((4,)), dma((4,)), dma((4,)),
-            dma((68,)), dma((68,)),
+            dma((32,)), dma((32,)),
         ],
         compiler_params=pltpu.CompilerParams(
             collective_id=0, has_side_effects=True, vmem_limit_bytes=62 << 20

time: 79.2 us -> 73.1 us (0.923)
  Pallas kernels: 78.4 us -> 72.3 us
    pallas_call x1, Pallas kernels: 76.6 us -> 70.5 us  [local(): pl.pallas_call(kernel, out_shape=(jax.ShapeDtypeStruct((512, D), BF), jax...]
where the time goes in v4:
time: 73.1 us; the launch traced here: 73 us
  Pallas kernels  72.3 us (99%)
    pallas_call x1, Pallas kernels, local(): pl.pallas_call(kernel, out_shape=(jax.ShapeDtypeStruct((512, D), BF), jax...  70.5 us
    pallas_call x1, Pallas kernels, local(): pl.pallas_call(finish, out_shape=(jax.ShapeDtypeStruct((512, D), BF), jax...  1.81 us

profile of v4, /device:TPU:1, one launch (start us, length us, event | category | flops | bytes accessed | tf_op | source)
XLA Modules:
  0.0 73.0 jit_solution(10432799268032298079)
XLA Ops:
  0.6 70.5 %shard_map.67 = (bf16[512,384]{1,0:T(8,128)(2,1)}, f32[2,48,256]{2,1,0:T(8,128)}) custom-call(bf16[512,384]{1,0:T(8,128)(2,1)} %sig.1, bf16[512,384]{1,0:T(8,128)(2,1)} %cot.1, bf16[768,1536]{1,0:T(8,128)(2,1)} %wu_hbm.1, bf16[768,1536]{1,0:T(8,128)(2,1)} %wd_hbm.1), custom_call_target="tpu_custom_call" | custom-call | tf_op jit(solution)/shard_map/pallas_call | solution.py:444
  71.2 1.8 %shard_map.68 = (bf16[512,384]{1,0:T(8,128)(2,1)}, f32[48,96]{1,0:T(8,128)}, f32[48,96]{1,0:T(8,128)}) custom-call(bf16[512,384]{1,0:T(8,128)(2,1)} %get-tuple-element.5.mixed, f32[2,48,256]{2,1,0:T(8,128)} %get-tuple-element.6.grads), custom_call_target="tpu_custom_call" | custom-call | tf_op jit(solution)/shard_map/pallas_call | solution.py:474

commit v5 on v4

--- a/solution.py
+++ b/solution.py
@@ -123,6 +123,11 @@
         cols = pl.ds(k * ROWS, ROWS)
         into = pl.ds(4 * ROWS + k * ROWS, ROWS)
         return remote(rk.at[1 - c, cols], rk.at[1 - c, into], rk_s.at[k], rk_r.at[k], other)
+
+    def send_right_part(p):
+        cols = pl.ds(p * 512, 512)
+        source = rk.at[1 - c, pl.ds(0, ROWS), cols]
+        return remote(source, rk.at[1 - c, pl.ds(4 * ROWS, ROWS), cols], rk_s.at[0], rk_r.at[0], other)
 
     for k in range(4):
         for i in range(8):
@@ -191,20 +196,35 @@
             gpv[rows, :D] = gs[low]
             gpv[rows, D:] = gs[high]
         mine = slice(k * ROWS, (k + 1) * ROWS)
+        if k == 0:
+            for j in range(3):
+                store_turned(1, j, mine, gpv)
+
+            @pl.when(c == 0)
+            def _():
+                send_left(k).start()
+
         for j in range(FF // TILE):
             cols = slice(j * TILE, (j + 1) * TILE)
             d_hidden = dot_nn(gpv[...], wd[:, cols])
             rk[0, mine, cols] = (d_hidden * slope[k, :, cols]).astype(BF)
-            if j < 3:
+            if k > 0 and j < 3:
                 store_turned(1, j, mine, gpv)
-
-        @pl.when(c == 0)
-        def _():
-            send_left(k).start()
-
-        @pl.when(c == 1)
-        def _():
-            send_right(k).start()
+            if k == 0 and j % 2 == 1:
+
+                @pl.when(c == 1)
+                def _():
+                    send_right_part(j // 2).start()
+
+        if k > 0:
+
+            @pl.when(c == 0)
+            def _():
+                send_left(k).start()
+
+            @pl.when(c == 1)
+            def _():
+                send_right(k).start()
 
         if k > 0:
             for j in range(D2 // TILE):
@@ -244,7 +264,7 @@
     def span(first, size=48):
         return pl.ds(first * 48, size)
 
-    a1 = [[link(sa1.at[i, d], ra1.at[i, d], ydev[d]) for d in range(2)] for i in range(4)]
+    a1 = [None] + [[link(sa1.at[i, d], ra1.at[i, d], ydev[d]) for d in range(2)] for i in range(1, 4)]
     a2n = [fresh() for i in range(4)]
     a2 = [
         [[link(sa2.at[i, d, span(h)], ra2.at[i, d, span(h)], ydev[d], a2n[i]) for h in range(2)] for d in range(2)]
@@ -255,7 +275,18 @@
     x2n, y2n, zn = fresh(), fresh(), fresh()
     x2 = [[link(sx2.at[d, span(h)], rx2.at[d, span(h)], xdev[d], x2n) for h in range(2)] for d in range(2)]
     x2_all = link(sx2, rx2, xdev[0], x2n)
-    b1 = [[link(sb1.at[d, g], rb1.at[d, g], xdev[d]) for g in range(4)] for d in range(2)]
+    parts = ((0, 256), (256, 128))
+
+    def pieces_of(whole, src, dst, dev):
+        n = fresh()
+        whole.append(link(src, dst, dev, n))
+        return [link(src.at[:, pl.ds(*p)], dst.at[:, pl.ds(*p)], dev, n) for p in parts]
+
+    a1_first, b1, b1_parts = [], [[], []], []
+    a1_parts = [pieces_of(a1_first, sa1.at[0, d], ra1.at[0, d], ydev[d]) for d in range(2)]
+    a1[0] = a1_first
+    for d in range(2):
+        b1_parts.append([pieces_of(b1[d], sb1.at[d, g], rb1.at[d, g], xdev[d]) for g in range(4)])
     b2n = [fresh() for g in range(4)]
     b2 = [
         [[link(sb2.at[d, g, span(h)], rb2.at[d, g, span(h)], xdev[d], b2n[g]) for h in range(2)] for g in range(4)]
@@ -283,10 +314,21 @@
         m4[i, :, 256:] = out[:, :128]
         m4[i + 1, :, 256:] = out[:, 128:]
 
+    def first_parts(p):
+        cols = slice(parts[p][0], sum(parts[p]))
+        for g in range(4):
+            for d in range(2):
+                sb1[d, g, :, cols] = m4[0, hrow(order[g], 2 + d), cols].astype(BF)
+                b1_parts[d][g][p].start()
+        for d in range(2):
+            sa1[0, d, :, cols] = m4[0, hrow(y2, d), cols].astype(BF)
+            a1_parts[d][p].start()
+
     def a_open(i):
         for d in range(2):
-            sa1[i, d] = m4[i, hrow(y2, d)].astype(BF)
-            a1[i][d].start()
+            if i > 0:
+                sa1[i, d] = m4[i, hrow(y2, d)].astype(BF)
+                a1[i][d].start()
         for d in range(2):
             sa2[i, d, (1 - d) * 48 : (2 - d) * 48] = m4[i, hrow(near[d], 1 - d)].astype(BF)
             a2[i][d][1 - d].start()
@@ -300,12 +342,6 @@
     def a_final(i):
         a2_all[i].wait()
         ay[i] = m4[i, mrow(y, 0)] + ra2[i, 0].astype(F32) + ra2[i, 1].astype(F32)
-
-    def b_open():
-        for g in range(4):
-            for d in range(2):
-                sb1[d, g] = m4[0, hrow(order[g], 2 + d)].astype(BF)
-                b1[d][g].start()
 
     def b_free(d, g):
         free = slice((1 - d) * 48, (2 - d) * 48)
@@ -337,8 +373,9 @@
         second[d][d].start()
 
     wide(0)
+    first_parts(0)
     shared(0)
-    b_open()
+    first_parts(1)
     a_open(0)
     wide(1)
     b_free(0, 0)
@@ -465,7 +502,7 @@
             vm((7, 48, 256), BF), vm((48, 256), F32), vm((48, 256), F32),
             dma((1,)), dma((1,)), dma((1,)), dma((1,)), dma((1,)), dma((1,)),
             dma((4,)), dma((4,)), dma((4,)), dma((4,)), dma((4,)),
-            dma((32,)), dma((32,)),
+            dma((34,)), dma((34,)),
         ],
         compiler_params=pltpu.CompilerParams(
             collective_id=0, has_side_effects=True, vmem_limit_bytes=62 << 20

time: 73.1 us -> 74.5 us (1.019)
  Pallas kernels: 72.3 us -> 73.8 us
    pallas_call x1, Pallas kernels: 70.5 us -> 72 us  [local(): pl.pallas_call(kernel, out_shape=(jax.ShapeDtypeStruct((512, D), BF), jax...]
where the time goes in v5:
time: 74.5 us; the launch traced here: 74.4 us
  Pallas kernels  73.8 us (99%)
    pallas_call x1, Pallas kernels, local(): pl.pallas_call(kernel, out_shape=(jax.ShapeDtypeStruct((512, D), BF), jax...  72 us
    pallas_call x1, Pallas kernels, local(): pl.pallas_call(finish, out_shape=(jax.ShapeDtypeStruct((512, D), BF), jax...  1.81 us

profile of v5, /device:TPU:1, one launch (start us, length us, event | category | flops | bytes accessed | tf_op | source)
XLA Modules:
  0.0 74.4 jit_solution(9468779118571352015)
XLA Ops:
  0.6 72.0 %shard_map.67 = (bf16[512,384]{1,0:T(8,128)(2,1)}, f32[2,48,256]{2,1,0:T(8,128)}) custom-call(bf16[512,384]{1,0:T(8,128)(2,1)} %sig.1, bf16[512,384]{1,0:T(8,128)(2,1)} %cot.1, bf16[768,1536]{1,0:T(8,128)(2,1)} %wu_hbm.1, bf16[768,1536]{1,0:T(8,128)(2,1)} %wd_hbm.1), custom_call_target="tpu_custom_call" | custom-call | tf_op jit(solution)/shard_map/pallas_call | solution.py:481
  72.6 1.8 %shard_map.68 = (bf16[512,384]{1,0:T(8,128)(2,1)}, f32[48,96]{1,0:T(8,128)}, f32[48,96]{1,0:T(8,128)}) custom-call(bf16[512,384]{1,0:T(8,128)(2,1)} %get-tuple-element.5.mixed, f32[2,48,256]{2,1,0:T(8,128)} %get-tuple-element.6.grads), custom_call_target="tpu_custom_call" | custom-call | tf_op jit(solution)/shard_map/pallas_call | solution.py:511

commit v6 on v4

--- a/solution.py
+++ b/solution.py
@@ -147,11 +147,6 @@
             slope[k, :, cols] = half
             if j % 2 == 1:
                 store_turned(0, j // 2, mine, nbv)
-
-        @pl.when(c == 0)
-        def _():
-            send_right(k).start()
-
         for j in range(D2 // TILE):
             cols = slice(j * TILE, (j + 1) * TILE)
             out = dot_nt(rk[1, mine], wd[cols])
@@ -172,6 +167,10 @@
         @pl.when(c == 1)
         def _():
             send_left(k).start()
+
+        @pl.when(c == 0)
+        def _():
+            send_right(k).start()
 
     mix_copies = []
     for r, dev, target in group:

time: 73.1 us -> 71.5 us (0.978)
  Pallas kernels: 72.3 us -> 70.7 us
    pallas_call x1, Pallas kernels: 70.5 us -> 68.9 us  [local(): pl.pallas_call(kernel, out_shape=(jax.ShapeDtypeStruct((512, D), BF), jax...]
where the time goes in v6:
time: 71.5 us; the launch traced here: 71.4 us
  Pallas kernels  70.7 us (99%)
    pallas_call x1, Pallas kernels, local(): pl.pallas_call(kernel, out_shape=(jax.ShapeDtypeStruct((512, D), BF), jax...  68.9 us
    pallas_call x1, Pallas kernels, local(): pl.pallas_call(finish, out_shape=(jax.ShapeDtypeStruct((512, D), BF), jax...  1.81 us

profile of v6, /device:TPU:1, one launch (start us, length us, event | category | flops | bytes accessed | tf_op | source)
XLA Modules:
  0.0 71.4 jit_solution(11294251138436017680)
XLA Ops:
  0.6 68.9 %shard_map.67 = (bf16[512,384]{1,0:T(8,128)(2,1)}, f32[2,48,256]{2,1,0:T(8,128)}) custom-call(bf16[512,384]{1,0:T(8,128)(2,1)} %sig.1, bf16[512,384]{1,0:T(8,128)(2,1)} %cot.1, bf16[768,1536]{1,0:T(8,128)(2,1)} %wu_hbm.1, bf16[768,1536]{1,0:T(8,128)(2,1)} %wd_hbm.1), custom_call_target="tpu_custom_call" | custom-call | tf_op jit(solution)/shard_map/pallas_call | solution.py:443
  69.6 1.8 %shard_map.68 = (bf16[512,384]{1,0:T(8,128)(2,1)}, f32[48,96]{1,0:T(8,128)}, f32[48,96]{1,0:T(8,128)}) custom-call(bf16[512,384]{1,0:T(8,128)(2,1)} %get-tuple-element.5.mixed, f32[2,48,256]{2,1,0:T(8,128)} %get-tuple-element.6.grads), custom_call_target="tpu_custom_call" | custom-call | tf_op jit(solution)/shard_map/pallas_call | solution.py:473
